TPU v7x, 512 devices: a whole 4x4x16 slice. The times are simulated.
512 devices in a mesh: section: 64 (over y, z_lo, core), coil: 8 (over z_hi, x).
Axes of the slice: x: 4, y: 4, z: 16 (z_hi: 2, z_lo: 8; z = z_hi * 8 + z_lo), core: 2. Of those that a mesh axis runs over, the one named last changes fastest.
Arguments:
- kspace: bfloat16 [16, 64, 64, 640], P('coil', None, 'section'), may hold values from -6 to 6
- coil_maps: bfloat16 [16, 64, 64, 640], P('coil', 'section'), may hold values from -1.5 to 1.5
- sampling: int32 [2, 32, 320], replicated, may hold values 0 or 1
- dc_weight: float32 [2], replicated, may hold values from 0.5 to 2.5
- kernel_in: float32 [2, 9, 18, 2], replicated, may hold values from -1.5 to 1.5
- bias_in: float32 [2, 18], replicated, may hold values from -0.5 to 0.5
- kernel_out: float32 [2, 9, 2, 18], replicated, may hold values from -0.5 to 0.5
- bias_out: float32 [2, 2], replicated, may hold values from -0.5 to 0.5
- cotangent: bfloat16 [64, 64, 640], P('section'), may hold values from -6 to 6
Outputs:
- image_out: float32 [64, 64, 640], P('section')
- grad_kspace: float32 [16, 64, 64, 640], P('coil', None, 'section')
All inputs are finite; a program needn't handle non-finite values.
Results may differ from a plain program's by a relative error of at most 0.035.
Values may be sent and summed in bfloat16 or wider, within the bound.
A program may use at most 64 MiB of HBM per device.

v0:
```python
import math

import jax
import jax.numpy as jnp
from jax import lax
from jax.sharding import PartitionSpec as P

CASCADES = 2
VOLUMES = 2


PRECISE = lax.Precision.HIGHEST


def line_table(count, exponent_sign):
    indices = jnp.arange(count, dtype=jnp.int32)
    product = indices[:, None] * indices[None, :] % count
    angles = product.astype(jnp.float32) * (2.0 * math.pi / count)
    factor = 1.0 / math.sqrt(count)
    return (jnp.cos(angles) * factor, exponent_sign * jnp.sin(angles) * factor)


def line_matrix(count, exponent_sign):
    real_part, imag_part = line_table(count, exponent_sign)
    upper_rows = jnp.concatenate([real_part, imag_part], axis=1)
    lower_rows = jnp.concatenate([-imag_part, real_part], axis=1)
    return jnp.concatenate([upper_rows, lower_rows], axis=0).astype(jnp.bfloat16)


def line_transform(values, matrix):
    return jnp.dot(values.astype(jnp.bfloat16), matrix, preferred_element_type=jnp.float32)


def depth_transform(values, volumes, exponent_sign):
    layout_shape = values.shape
    width_two = layout_shape[-1]
    half_width = width_two // 2
    depth_count = layout_shape[1] // volumes
    real_part, imag_part = line_table(depth_count, exponent_sign)
    blocks = values.astype(jnp.bfloat16).reshape(
        layout_shape[0], volumes, depth_count, layout_shape[2], width_two
    )
    straight = jnp.einsum(
        "kz,cvzrw->cvkrw",
        real_part.astype(jnp.bfloat16),
        blocks,
        preferred_element_type=jnp.float32,
    )
    crossed = jnp.einsum(
        "kz,cvzrw->cvkrw",
        imag_part.astype(jnp.bfloat16),
        blocks,
        preferred_element_type=jnp.float32,
    )
    turned = jnp.concatenate([-crossed[..., half_width:], crossed[..., :half_width]], axis=-1)
    return (straight + turned).reshape(layout_shape)


def spread(coil_maps, picture):
    half_width = coil_maps.shape[-1] // 2
    maps_real = coil_maps[..., :half_width].astype(jnp.float32)
    maps_imag = coil_maps[..., half_width:].astype(jnp.float32)
    pic_real = picture[..., :half_width].astype(jnp.float32)
    pic_imag = picture[..., half_width:].astype(jnp.float32)
    return jnp.concatenate(
        [maps_real * pic_real - maps_imag * pic_imag, maps_real * pic_imag + maps_imag * pic_real],
        axis=-1,
    )


def collect(coil_maps, coil_images):
    half_width = coil_maps.shape[-1] // 2
    maps_real = coil_maps[..., :half_width].astype(jnp.float32)
    maps_imag = coil_maps[..., half_width:].astype(jnp.float32)
    img_real = coil_images[..., :half_width]
    img_imag = coil_images[..., half_width:]
    summed = jnp.concatenate(
        [maps_real * img_real + maps_imag * img_imag, maps_real * img_imag - maps_imag * img_real],
        axis=-1,
    )
    return jnp.sum(summed, axis=0)


def shifted_windows(planes):
    row_count, col_count = (planes.shape[-2], planes.shape[-1])
    padded = jnp.pad(planes, ((0, 0), (1, 1), (1, 1)))
    return jnp.stack(
        [
            padded[:, row_shift : row_shift + row_count, col_shift : col_shift + col_count]
            for row_shift in range(3)
            for col_shift in range(3)
        ],
        axis=0,
    )


def conv_out(hidden, kernel, bias):
    row_count, col_count = (hidden.shape[-2], hidden.shape[-1])
    projected = jnp.einsum("toc,cxy->toxy", kernel, hidden, precision=PRECISE)
    padded = jnp.pad(projected, ((0, 0), (0, 0), (1, 1), (1, 1)))
    summed = jnp.zeros((kernel.shape[1], row_count, col_count), jnp.float32) + bias[:, None, None]
    for tap_index in range(9):
        row_shift = tap_index // 3
        col_shift = tap_index % 3
        summed = (
            summed
            + padded[
                tap_index, :, row_shift : row_shift + row_count, col_shift : col_shift + col_count
            ]
        )
    return summed


def refine(picture, kernel_in, bias_in, kernel_out, bias_out):
    half_width = picture.shape[-1] // 2
    planes = jnp.stack([picture[:, :half_width], picture[:, half_width:]], axis=0)
    hidden = (
        jnp.einsum("toc,tcxy->oxy", kernel_in, shifted_windows(planes), precision=PRECISE)
        + bias_in[:, None, None]
    )
    hidden = jax.nn.silu(hidden)
    output = conv_out(hidden, kernel_out, bias_out)
    return jnp.concatenate([output[0], output[1]], axis=1)


def body(
    kspace, coil_maps, sampling, dc_weight, kernel_in, bias_in, kernel_out, bias_out, cotangent
):
    width_two = kspace.shape[-1]
    slot_count = kspace.shape[1]
    lines_used = sampling.astype(jnp.float32).reshape(slot_count, width_two // 2)
    sampled = jnp.concatenate([lines_used, lines_used], axis=1)[None, :, None, :]
    measured = sampled * kspace.astype(jnp.float32)
    forward_line = line_matrix(width_two // 2, -1.0)
    inverse_line = line_matrix(width_two // 2, 1.0)

    def expand(picture):
        spreaded = spread(coil_maps, picture[None])
        line_out = line_transform(spreaded, forward_line).astype(jnp.bfloat16)
        moved = lax.all_to_all(line_out, "section", split_axis=2, concat_axis=1, tiled=True)
        return depth_transform(moved, VOLUMES, -1.0)

    def combine(kstate, is_final):
        depth_out = depth_transform(kstate, VOLUMES, 1.0).astype(jnp.bfloat16)
        moved = lax.all_to_all(depth_out, "section", split_axis=1, concat_axis=2, tiled=True)
        partial_sum = collect(coil_maps, line_transform(moved, inverse_line))
        summed = lax.psum(partial_sum.astype(jnp.bfloat16), "coil").astype(jnp.float32)
        if is_final:
            return summed
        return summed.astype(jnp.bfloat16)

    kstate = measured
    stored = []
    for cascade in range(CASCADES):
        picture = combine(kstate, False)[0].astype(jnp.float32)
        stored.append(picture)
        model = refine(
            picture, kernel_in[cascade], bias_in[cascade], kernel_out[cascade], bias_out[cascade]
        )
        update = expand(model.astype(jnp.bfloat16)[None])
        kstate = kstate - dc_weight[cascade] * sampled * (kstate - measured) + update
    image_out = combine(kstate, True)
    adjoint = expand(cotangent)
    grad_measured = jnp.zeros(measured.shape, jnp.float32)
    for cascade in reversed(range(CASCADES)):
        weighted = dc_weight[cascade] * sampled
        grad_measured = grad_measured + weighted * adjoint
        model_bar = combine(adjoint, False)[0].astype(jnp.float32)
        adjoint = adjoint - weighted * adjoint

        def local_model(flat, index=cascade):
            return refine(
                flat, kernel_in[index], bias_in[index], kernel_out[index], bias_out[index]
            )

        unused, pull_back = jax.vjp(local_model, stored[cascade])
        picture_bar = pull_back(model_bar)[0]
        adjoint = adjoint + expand(picture_bar.astype(jnp.bfloat16)[None])
    grad_measured = grad_measured + adjoint
    return (image_out, sampled * grad_measured)


def solution(mesh):
    return jax.shard_map(
        body,
        mesh=mesh,
        in_specs=(
            P("coil", None, "section", None),
            P("coil", "section", None, None),
            P(),
            P(),
            P(),
            P(),
            P(),
            P(),
            P("section", None, None),
        ),
        out_specs=(P("section", None, None), P("coil", None, "section", None)),
        check_vma=False,
    )
```

profile of v0, /device:TPU:1, one launch (start us, length us, event | category | flops | bytes accessed | tf_op | source)
XLA Modules:
  0.0 784.4 jit_solution(11465072695413646066)
XLA Ops:
  14.4 17.3 %all-to-all-start = ((bf16[2,64,1,640]{3,0,2,1:T(2,128)(2,1)}), bf16[2,64,1,640]{3,0,2,1:T(2,128)(2,1)S(1)}, u32[]{:S(2)}, u32[]{:S(2)}) async-start(bf16[2,64,1,640]{3,0,2,1:T(2,128)(2,1)} %copy.66), calls=%async_computation | async-start | bytes 327680 | tf_op jit(solution)/shard_map/all_to_all | solution.py:145
  36.8 10.5 %all-to-all-done = bf16[2,64,1,640]{3,0,2,1:T(2,128)(2,1)S(1)} async-done(((bf16[2,64,1,640]{3,0,2,1:T(2,128)(2,1)}), bf16[2,64,1,640]{3,0,2,1:T(2,128)(2,1)S(1)}, u32[]{:S(2)}, u32[]{:S(2)}) %all-to-all-start) | async-done | bytes 163872 | tf_op jit(solution)/shard_map/all_to_all | solution.py:145
  48.7 2.7 negate_convert_fusion
  51.4 131.9 %all-reduce.54.cloned.1.call-done = bf16[64,640]{1,0:T(8,128)(2,1)} async-done(((bf16[64,640]{1,0:T(8,128)(2,1)}), bf16[64,640]{1,0:T(8,128)(2,1)}) %all-reduce.54.cloned.1.call-update) | async-done | bytes 81936 | tf_op jit(solution)/shard_map/psum | solution.py:147
  194.6 7.2 stack.116
  205.6 3.3 fusion.34
  213.1 9.9 %all-to-all-start.5 = ((bf16[2,1,64,640]{3,0,1,2:T(2,128)(2,1)}), bf16[2,1,64,640]{3,0,1,2:T(2,128)(2,1)S(1)}, u32[]{:S(2)}, u32[]{:S(2)}) async-start(bf16[2,1,64,640]{3,0,1,2:T(2,128)(2,1)} %copy.103), calls=%async_computation.5 | async-start | bytes 327680 | tf_op jit(solution)/shard_map/all_to_all | solution.py:140
  224.3 14.3 %all-to-all-done.5 = bf16[2,1,64,640]{3,0,1,2:T(2,128)(2,1)S(1)} async-done(((bf16[2,1,64,640]{3,0,1,2:T(2,128)(2,1)}), bf16[2,1,64,640]{3,0,1,2:T(2,128)(2,1)S(1)}, u32[]{:S(2)}, u32[]{:S(2)}) %all-to-all-start.5) | async-done | bytes 163872 | tf_op jit(solution)/shard_map/all_to_all | solution.py:140
  238.5 6.7 all-to-all-start.1
  247.7 12.9 %all-to-all-done.1 = bf16[2,1,64,640]{3,0,1,2:T(2,128)(2,1)S(1)} async-done(((bf16[2,1,64,640]{3,0,1,2:T(2,128)(2,1)}), bf16[2,1,64,640]{3,0,1,2:T(2,128)(2,1)S(1)}, u32[]{:S(2)}, u32[]{:S(2)}) %all-to-all-start.1) | async-done | bytes 163872 | tf_op jit(solution)/shard_map/all_to_all | solution.py:140
  260.7 6.5 all-to-all-start.6
  270.7 12.0 %all-to-all-done.6 = bf16[2,64,1,640]{3,0,2,1:T(2,128)(2,1)S(1)} async-done(((bf16[2,64,1,640]{3,0,2,1:T(2,128)(2,1)}), bf16[2,64,1,640]{3,0,2,1:T(2,128)(2,1)S(1)}, u32[]{:S(2)}, u32[]{:S(2)}) %all-to-all-start.6) | async-done | bytes 163872 | tf_op jit(solution)/shard_map/all_to_all | solution.py:145
  282.7 6.5 all-to-all-start.2
  289.6 15.1 %all-to-all-done.2 = bf16[2,64,1,640]{3,0,2,1:T(2,128)(2,1)S(1)} async-done(((bf16[2,64,1,640]{3,0,2,1:T(2,128)(2,1)}), bf16[2,64,1,640]{3,0,2,1:T(2,128)(2,1)S(1)}, u32[]{:S(2)}, u32[]{:S(2)}) %all-to-all-start.2) | async-done | bytes 163872 | tf_op jit(solution)/shard_map/all_to_all | solution.py:145
  306.9 140.1 %all-reduce.58.cloned.1.call-done = (bf16[64,640]{1,0:T(8,128)(2,1)}, bf16[64,640]{1,0:T(8,128)(2,1)}) async-done(((bf16[64,640]{1,0:T(8,128)(2,1)}, bf16[64,640]{1,0:T(8,128)(2,1)}), (bf16[64,640]{1,0:T(8,128)(2,1)}, bf16[64,640]{1,0:T(8,128)(2,1)})) %all-reduce.58.cloned.1.call-update) | async-done | bytes 163856 | tf_op jit(solution)/shard_map/psum | solution.py:147
  461.4 6.9 stack.129
  470.6 3.3 fusion.37
  477.1 6.6 fusion.2
  483.8 4.1 fusion.31
  495.2 11.3 %all-to-all-start.7 = ((bf16[2,1,64,640]{3,0,1,2:T(2,128)(2,1)}), bf16[2,1,64,640]{3,0,1,2:T(2,128)(2,1)S(1)}, u32[]{:S(2)}, u32[]{:S(2)}) async-start(bf16[2,1,64,640]{3,0,1,2:T(2,128)(2,1)} %copy.119), calls=%async_computation.7 | async-start | bytes 327680 | tf_op jit(solution)/shard_map/all_to_all | solution.py:140
  508.6 13.5 %all-to-all-done.7 = bf16[2,1,64,640]{3,0,1,2:T(2,128)(2,1)S(1)} async-done(((bf16[2,1,64,640]{3,0,1,2:T(2,128)(2,1)}), bf16[2,1,64,640]{3,0,1,2:T(2,128)(2,1)S(1)}, u32[]{:S(2)}, u32[]{:S(2)}) %all-to-all-start.7) | async-done | bytes 163872 | tf_op jit(solution)/shard_map/all_to_all | solution.py:140
  522.1 6.5 all-to-all-start.3
  530.8 13.3 %all-to-all-done.3 = bf16[2,1,64,640]{3,0,1,2:T(2,128)(2,1)S(1)} async-done(((bf16[2,1,64,640]{3,0,1,2:T(2,128)(2,1)}), bf16[2,1,64,640]{3,0,1,2:T(2,128)(2,1)S(1)}, u32[]{:S(2)}, u32[]{:S(2)}) %all-to-all-start.3) | async-done | bytes 163872 | tf_op jit(solution)/shard_map/all_to_all | solution.py:140
  544.1 6.5 all-to-all-start.8
  553.4 12.7 %all-to-all-done.8 = bf16[2,64,1,640]{3,0,2,1:T(2,128)(2,1)S(1)} async-done(((bf16[2,64,1,640]{3,0,2,1:T(2,128)(2,1)}), bf16[2,64,1,640]{3,0,2,1:T(2,128)(2,1)S(1)}, u32[]{:S(2)}, u32[]{:S(2)}) %all-to-all-start.8) | async-done | bytes 163872 | tf_op jit(solution)/shard_map/all_to_all | solution.py:145
  566.1 6.5 all-to-all-start.4
  573.2 14.9 %all-to-all-done.4 = bf16[2,64,1,640]{3,0,2,1:T(2,128)(2,1)S(1)} async-done(((bf16[2,64,1,640]{3,0,2,1:T(2,128)(2,1)}), bf16[2,64,1,640]{3,0,2,1:T(2,128)(2,1)S(1)}, u32[]{:S(2)}, u32[]{:S(2)}) %all-to-all-start.4) | async-done | bytes 163872 | tf_op jit(solution)/shard_map/all_to_all | solution.py:145
  590.3 138.2 %all-reduce.56.cloned.1.call-done = (bf16[1,64,640]{2,1,0:T(8,128)(2,1)}, bf16[64,640]{1,0:T(8,128)(2,1)}) async-done(((bf16[1,64,640]{2,1,0:T(8,128)(2,1)}, bf16[64,640]{1,0:T(8,128)(2,1)}), (bf16[1,64,640]{2,1,0:T(8,128)(2,1)}, bf16[64,640]{1,0:T(8,128)(2,1)})) %all-reduce.56.cloned.1.call-update) | async-done | bytes 163856 | tf_op jit(solution)/shard_map/psum | solution.py:147
  732.2 6.2 fusion
  738.4 4.4 fusion.28
  748.4 11.3 %all-to-all-start.9 = ((bf16[2,1,64,640]{3,0,1,2:T(2,128)(2,1)}), bf16[2,1,64,640]{3,0,1,2:T(2,128)(2,1)S(1)}, u32[]{:S(2)}, u32[]{:S(2)}) async-start(bf16[2,1,64,640]{3,0,1,2:T(2,128)(2,1)} %copy.134), calls=%async_computation.9 | async-start | bytes 327680 | tf_op jit(solution)/shard_map/all_to_all | solution.py:140
  760.4 14.9 %all-to-all-done.9 = bf16[2,1,64,640]{3,0,1,2:T(2,128)(2,1)S(1)} async-done(((bf16[2,1,64,640]{3,0,1,2:T(2,128)(2,1)}), bf16[2,1,64,640]{3,0,1,2:T(2,128)(2,1)S(1)}, u32[]{:S(2)}, u32[]{:S(2)}) %all-to-all-start.9) | async-done | bytes 163872 | tf_op jit(solution)/shard_map/all_to_all | solution.py:140
  (260 shorter events, 91.1 us)
Async XLA Ops:
  11.6 24.3 %copy-start.33 = (f32[2,9,18,2]{2,3,1,0:T(2,128)S(1)}, f32[2,9,18,2]{2,3,1,0:T(2,128)}, u32[]{:S(2)}) copy-start(f32[2,9,18,2]{2,3,1,0:T(2,128)} %param.13) | copy-start | bytes 7780
  11.6 24.4 %copy-start.35 = (f32[2,18]{1,0:T(2,128)S(1)}, f32[2,18]{1,0:T(2,128)}, u32[]{:S(2)}) copy-start(f32[2,18]{1,0:T(2,128)} %param.14) | copy-start | bytes 436
  11.6 24.4 %copy-start.36 = (f32[2,2]{1,0:T(2,128)S(1)}, f32[2,2]{1,0:T(2,128)}, u32[]{:S(2)}) copy-start(f32[2,2]{1,0:T(2,128)} %param.16) | copy-start | bytes 52
  11.6 24.4 %copy-start.34 = (f32[2,9,2,18]{3,2,1,0:T(2,128)S(1)}, f32[2,9,2,18]{3,2,1,0:T(2,128)}, u32[]{:S(2)}) copy-start(f32[2,9,2,18]{3,2,1,0:T(2,128)} %param.15) | copy-start | bytes 7780
  11.7 24.4 %copy-start.31 = (bf16[1,64,640]{2,1,0:T(8,128)(2,1)S(1)}, bf16[1,64,640]{2,1,0:T(8,128)(2,1)}, u32[]{:S(2)}) copy-start(bf16[1,64,640]{2,1,0:T(8,128)(2,1)} %param.17) | copy-start | bytes 245764
  14.4 33.3 %copy-start = (bf16[2,1,64,640]{3,2,1,0:T(8,128)(2,1)S(1)}, bf16[2,1,64,640]{3,2,1,0:T(8,128)(2,1)}, u32[]{:S(2)}) copy-start(bf16[2,1,64,640]{3,2,1,0:T(8,128)(2,1)} %param.10) | copy-start | bytes 491524
  14.4 32.9 %all-to-all-start = ((bf16[2,64,1,640]{3,0,2,1:T(2,128)(2,1)}), bf16[2,64,1,640]{3,0,2,1:T(2,128)(2,1)S(1)}, u32[]{:S(2)}, u32[]{:S(2)}) async-start(bf16[2,64,1,640]{3,0,2,1:T(2,128)(2,1)} %copy.66), calls=%async_computation | async-start | bytes 327680 | tf_op jit(solution)/shard_map/all_to_all | solution.py:145
  31.8 151.5 %all-reduce.54.cloned.1.call-start = ((), (), s32[]{:S(2)}) async-start(), calls=%async_computation.10 | async-start | bytes 163840 | tf_op jit(solution)/shard_map/psum | solution.py:147
  34.0 13.9 %copy-start.18 = (bf16[320,320]{1,0:T(8,128)(2,1)}, bf16[320,320]{1,0:T(8,128)(2,1)S(1)}, u32[]{:S(2)}) copy-start(bf16[320,320]{1,0:T(8,128)(2,1)S(1)} %get-tuple-element.122) | copy-start | bytes 614404
  213.1 25.5 %all-to-all-start.5 = ((bf16[2,1,64,640]{3,0,1,2:T(2,128)(2,1)}), bf16[2,1,64,640]{3,0,1,2:T(2,128)(2,1)S(1)}, u32[]{:S(2)}, u32[]{:S(2)}) async-start(bf16[2,1,64,640]{3,0,1,2:T(2,128)(2,1)} %copy.103), calls=%async_computation.5 | async-start | bytes 327680 | tf_op jit(solution)/shard_map/all_to_all | solution.py:140
  238.5 22.2 %all-to-all-start.1 = ((bf16[2,1,64,640]{3,0,1,2:T(2,128)(2,1)}), bf16[2,1,64,640]{3,0,1,2:T(2,128)(2,1)S(1)}, u32[]{:S(2)}, u32[]{:S(2)}) async-start(bf16[2,1,64,640]{3,0,1,2:T(2,128)(2,1)} %copy.81), calls=%async_computation.1 | async-start | bytes 327680 | tf_op jit(solution)/shard_map/all_to_all | solution.py:140
  246.2 21.6 %copy-start.7 = (f32[64,640]{1,0:T(8,128)S(1)}, f32[64,640]{1,0:T(8,128)}, u32[]{:S(2)}) copy-start(f32[64,640]{1,0:T(8,128)} %get-tuple-element.99) | copy-start | bytes 491524
  246.2 21.6 %copy-start.9 = (bf16[2,64,1,640]{3,1,2,0:T(8,128)(2,1)S(1)}, bf16[2,64,1,640]{3,1,2,0:T(8,128)(2,1)}, u32[]{:S(2)}) copy-start(bf16[2,64,1,640]{3,1,2,0:T(8,128)(2,1)} %param.9) | copy-start | bytes 491524
  260.7 22.0 %all-to-all-start.6 = ((bf16[2,64,1,640]{3,0,2,1:T(2,128)(2,1)}), bf16[2,64,1,640]{3,0,2,1:T(2,128)(2,1)S(1)}, u32[]{:S(2)}, u32[]{:S(2)}) async-start(bf16[2,64,1,640]{3,0,2,1:T(2,128)(2,1)} %copy.107), calls=%async_computation.6 | async-start | bytes 327680 | tf_op jit(solution)/shard_map/all_to_all | solution.py:145
  267.8 21.4 %copy-start.26 = (bf16[320,320]{1,0:T(8,128)(2,1)S(1)}, bf16[320,320]{1,0:T(8,128)(2,1)}, u32[]{:S(2)}) copy-start(bf16[320,320]{1,0:T(8,128)(2,1)} %copy-done.25) | copy-start | bytes 614404
  267.8 21.4 %copy-start.29 = (bf16[320,320]{1,0:T(8,128)(2,1)S(1)}, bf16[320,320]{1,0:T(8,128)(2,1)}, u32[]{:S(2)}) copy-start(bf16[320,320]{1,0:T(8,128)(2,1)} %copy-done.28) | copy-start | bytes 614404
  282.7 22.0 %all-to-all-start.2 = ((bf16[2,64,1,640]{3,0,2,1:T(2,128)(2,1)}), bf16[2,64,1,640]{3,0,2,1:T(2,128)(2,1)S(1)}, u32[]{:S(2)}, u32[]{:S(2)}) async-start(bf16[2,64,1,640]{3,0,2,1:T(2,128)(2,1)} %copy.84), calls=%async_computation.2 | async-start | bytes 327680 | tf_op jit(solution)/shard_map/all_to_all | solution.py:145
  289.2 157.8 %all-reduce.58.cloned.1.call-start = ((), (), s32[]{:S(2)}) async-start(), calls=%async_computation.12 | async-start | bytes 327680 | tf_op jit(solution)/shard_map/psum | solution.py:147
  495.2 26.8 %all-to-all-start.7 = ((bf16[2,1,64,640]{3,0,1,2:T(2,128)(2,1)}), bf16[2,1,64,640]{3,0,1,2:T(2,128)(2,1)S(1)}, u32[]{:S(2)}, u32[]{:S(2)}) async-start(bf16[2,1,64,640]{3,0,1,2:T(2,128)(2,1)} %copy.119), calls=%async_computation.7 | async-start | bytes 327680 | tf_op jit(solution)/shard_map/all_to_all | solution.py:140
  507.7 21.4 %copy-start.2 = (f32[2,2,32,1,640]{4,2,1,0,3:T(8,128)S(1)}, f32[2,2,32,1,640]{4,2,1,0,3:T(8,128)}, u32[]{:S(2)}) copy-start(f32[2,2,32,1,640]{4,2,1,0,3:T(8,128)} %copy-done.1) | copy-start | bytes 983044
  522.1 22.0 %all-to-all-start.3 = ((bf16[2,1,64,640]{3,0,1,2:T(2,128)(2,1)}), bf16[2,1,64,640]{3,0,1,2:T(2,128)(2,1)S(1)}, u32[]{:S(2)}, u32[]{:S(2)}) async-start(bf16[2,1,64,640]{3,0,1,2:T(2,128)(2,1)} %copy.98), calls=%async_computation.3 | async-start | bytes 327680 | tf_op jit(solution)/shard_map/all_to_all | solution.py:140
  529.5 21.7 %copy-start.5 = (f32[64,640]{1,0:T(8,128)S(1)}, f32[64,640]{1,0:T(8,128)}, u32[]{:S(2)}) copy-start(f32[64,640]{1,0:T(8,128)} %get-tuple-element.98) | copy-start | bytes 491524
  529.5 21.7 %copy-start.10 = (bf16[2,64,1,640]{3,1,2,0:T(8,128)(2,1)S(1)}, bf16[2,64,1,640]{3,1,2,0:T(8,128)(2,1)}, u32[]{:S(2)}) copy-start(bf16[2,64,1,640]{3,1,2,0:T(8,128)(2,1)} %param.9) | copy-start | bytes 491524
  529.5 21.7 %copy-start.11 = (f32[2,64,1,640]{3,2,1,0:T(1,128)S(1)}, f32[2,64,1,640]{3,2,1,0:T(1,128)}, u32[]{:S(2)}) copy-start(f32[2,64,1,640]{3,2,1,0:T(1,128)} %get-tuple-element.7) | copy-start | bytes 983044
  544.1 22.0 %all-to-all-start.8 = ((bf16[2,64,1,640]{3,0,2,1:T(2,128)(2,1)}), bf16[2,64,1,640]{3,0,2,1:T(2,128)(2,1)S(1)}, u32[]{:S(2)}, u32[]{:S(2)}) async-start(bf16[2,64,1,640]{3,0,2,1:T(2,128)(2,1)} %copy.122), calls=%async_computation.8 | async-start | bytes 327680 | tf_op jit(solution)/shard_map/all_to_all | solution.py:145
  551.2 21.6 %copy-start.27 = (bf16[320,320]{1,0:T(8,128)(2,1)S(1)}, bf16[320,320]{1,0:T(8,128)(2,1)}, u32[]{:S(2)}) copy-start(bf16[320,320]{1,0:T(8,128)(2,1)} %copy-done.25) | copy-start | bytes 614404
  551.2 21.6 %copy-start.30 = (bf16[320,320]{1,0:T(8,128)(2,1)S(1)}, bf16[320,320]{1,0:T(8,128)(2,1)}, u32[]{:S(2)}) copy-start(bf16[320,320]{1,0:T(8,128)(2,1)} %copy-done.28) | copy-start | bytes 614404
  566.1 22.0 %all-to-all-start.4 = ((bf16[2,64,1,640]{3,0,2,1:T(2,128)(2,1)}), bf16[2,64,1,640]{3,0,2,1:T(2,128)(2,1)S(1)}, u32[]{:S(2)}, u32[]{:S(2)}) async-start(bf16[2,64,1,640]{3,0,2,1:T(2,128)(2,1)} %copy.101), calls=%async_computation.4 | async-start | bytes 327680 | tf_op jit(solution)/shard_map/all_to_all | solution.py:145
  572.5 155.9 %all-reduce.56.cloned.1.call-start = ((), (), s32[]{:S(2)}) async-start(), calls=%async_computation.11 | async-start | bytes 327680 | tf_op jit(solution)/shard_map/psum | solution.py:147
  747.5 28.4 %copy-start.6 = (f32[64,640]{1,0:T(8,128)S(1)}, f32[64,640]{1,0:T(8,128)}, u32[]{:S(2)}) copy-start(f32[64,640]{1,0:T(8,128)} %get-tuple-element.98) | copy-start | bytes 491524
  747.5 28.4 %copy-start.8 = (f32[64,640]{1,0:T(8,128)S(1)}, f32[64,640]{1,0:T(8,128)}, u32[]{:S(2)}) copy-start(f32[64,640]{1,0:T(8,128)} %get-tuple-element.99) | copy-start | bytes 491524
  748.4 26.8 %all-to-all-start.9 = ((bf16[2,1,64,640]{3,0,1,2:T(2,128)(2,1)}), bf16[2,1,64,640]{3,0,1,2:T(2,128)(2,1)S(1)}, u32[]{:S(2)}, u32[]{:S(2)}) async-start(bf16[2,1,64,640]{3,0,1,2:T(2,128)(2,1)} %copy.134), calls=%async_computation.9 | async-start | bytes 327680 | tf_op jit(solution)/shard_map/all_to_all | solution.py:140
  (18 other events, 80.4 us)
Sparse Core Ops, SparseCore 0:
  48.8 134.4 all-reduce.53
  307.0 139.9 all-reduce.57
  590.4 137.9 all-reduce.55
where the time goes:
time: 793 us; the launch traced here: 784 us
  waiting for transfers between devices  544 us (69%)
  starting transfers between devices  89.2 us (11%)
  local copies, waits for them, and re-layouts  56.7 us (7%)
  matrix products  41.8 us (5%)
  other arithmetic  36.8 us (5%)
  between operations  15.8 us (2%)
    psum x3, waiting for transfers between devices, combine(): lax.psum(partial_sum.astype(jnp.bfloat16), 'coil').astype(jnp.float32)  410 us
    all_to_all x5, waiting for transfers between devices, expand(): lax.all_to_all(line_out, 'section', split_axis=2, concat_axis=1, tiled=True)  68.9 us
    all_to_all x5, waiting for transfers between devices, combine(): lax.all_to_all(depth_out, 'section', split_axis=1, concat_axis=2, tiled=T...  65.1 us
    all_to_all x5, starting transfers between devices, expand(): lax.all_to_all(line_out, 'section', split_axis=2, concat_axis=1, tiled=True)  45.7 us
    all_to_all x5, starting transfers between devices, combine(): lax.all_to_all(depth_out, 'section', split_axis=1, concat_axis=2, tiled=T...  43.1 us
    another operation x22, local copies, waits for them, and re-layouts, shifted_windows(): jnp.stack([padded[:, row_shift:row_shift + row_count, col_shift:col_shift...  32.1 us
    dot_general x4, matrix products, conv_out(): projected = jnp.einsum('toc,cxy->toxy', kernel, hidden, precision=PRECISE)  19.3 us
  transfers between devices with their start and end apart: 13, of which 13 were waited for; matrix products, arithmetic and copies ran while one was open for 3% of the time, Pallas kernels for 0%

commit v1 on v0

v1 whole, which is shorter than its diff:
```python
import functools
import math

import jax
import jax.numpy as jnp
import numpy as np
from jax import lax
from jax.experimental import pallas as pl
from jax.experimental.pallas import tpu as pltpu
from jax.sharding import PartitionSpec as P

BF = jnp.bfloat16
F32 = jnp.float32
HID = 18
WIDE = 384
ROWPAD = 8


def tables(count, wide):
    index = np.arange(count)
    angle = (index[:, None] * index[None, :] % count) * (2.0 * math.pi / count)
    cosine = np.zeros((wide, wide), np.float32)
    sine = np.zeros((wide, wide), np.float32)
    cosine[:count, :count] = np.cos(angle) / math.sqrt(count)
    sine[:count, :count] = np.sin(angle) / math.sqrt(count)
    return cosine, sine


def line_tables(count):
    cosine, sine = tables(count, WIDE)
    return jnp.asarray(cosine).astype(BF), jnp.asarray(sine).astype(BF)


def depth_tables(depth, blocks):
    cosine, sine = tables(depth, depth)
    eye = np.eye(blocks, dtype=np.float32)
    return jnp.asarray(np.kron(eye, cosine)).astype(BF), jnp.asarray(np.kron(eye, sine)).astype(BF)


def dot(a, b):
    return jnp.dot(a, b, preferred_element_type=F32)


def line_transform(real, imag, cosine, sine, sign):
    rows = real.shape[0]
    both = jnp.concatenate([real, imag], axis=0).astype(BF)
    straight = dot(both, cosine)
    crossed = dot(both, sine)
    return straight[:rows] - sign * crossed[rows:], straight[rows:] + sign * crossed[:rows]


def depth_transform(real, imag, cosine, sine, sign):
    both = jnp.concatenate([real, imag], axis=1).astype(BF)
    straight = dot(cosine, both)
    crossed = dot(sine, both)
    return (
        straight[:, :WIDE] - sign * crossed[:, WIDE:],
        straight[:, WIDE:] + sign * crossed[:, :WIDE],
    )


class Row:
    def __init__(self, maps, mask, cosine, sine, zcos, zsin, slots):
        self.maps_real = maps[:, :WIDE].astype(F32)
        self.maps_imag = maps[:, WIDE:].astype(F32)
        self.coils = maps.shape[0] // slots
        self.mask = jnp.concatenate([mask] * self.coils, axis=0)
        self.line = (cosine, sine)
        self.depth = (zcos, zsin)
        self.slots = slots

    def expand(self, picture):
        real = jnp.concatenate([picture[:, :WIDE].astype(F32)] * self.coils, axis=0)
        imag = jnp.concatenate([picture[:, WIDE:].astype(F32)] * self.coils, axis=0)
        out = (
            self.maps_real * real - self.maps_imag * imag,
            self.maps_real * imag + self.maps_imag * real,
        )
        out = line_transform(*out, *self.line, -1.0)
        return depth_transform(*out, *self.depth, -1.0)

    def combine(self, real, imag):
        real, imag = depth_transform(real, imag, *self.depth, 1.0)
        real, imag = line_transform(real, imag, *self.line, 1.0)
        out_real = self.maps_real * real + self.maps_imag * imag
        out_imag = self.maps_real * imag - self.maps_imag * real
        n = self.slots
        return (
            sum(out_real[c * n : c * n + n] for c in range(self.coils)),
            sum(out_imag[c * n : c * n + n] for c in range(self.coils)),
        )

    def normal(self, picture):
        real, imag = self.expand(picture)
        return self.combine(self.mask * real, self.mask * imag)


def start_kernel(weight_ref, k_ref, maps_ref, cot_ref, mask_ref, c_ref, s_ref, zc_ref, zs_ref, y_ref, d_ref):
    slots = cot_ref.shape[0]
    row = Row(maps_ref[...], mask_ref[...], c_ref[...], s_ref[...], zc_ref[...], zs_ref[...], slots)
    weighted = weight_ref[0] * row.mask
    start = []
    for part in (0, 1):
        measured = row.mask * k_ref[:, part * WIDE : part * WIDE + WIDE].astype(F32)
        start.append(measured - weighted * (measured - measured))
    real, imag = row.combine(*start)
    y_ref[:, :WIDE] = real.astype(BF)
    y_ref[:, WIDE:] = imag.astype(BF)
    real, imag = row.normal(cot_ref[...])
    d_ref[:, :WIDE] = real.astype(BF)
    d_ref[:, WIDE:] = imag.astype(BF)


def normal_kernel(maps_ref, pic_ref, mask_ref, c_ref, s_ref, zc_ref, zs_ref, d_ref):
    slots = pic_ref.shape[0]
    row = Row(maps_ref[...], mask_ref[...], c_ref[...], s_ref[...], zc_ref[...], zs_ref[...], slots)
    real, imag = row.normal(pic_ref[...])
    d_ref[:, :WIDE] = real.astype(BF)
    d_ref[:, WIDE:] = imag.astype(BF)


def final_kernel(maps_ref, pic_ref, mask_ref, c_ref, s_ref, zc_ref, zs_ref, g_ref):
    slots = pic_ref.shape[0]
    row = Row(maps_ref[...], mask_ref[...], c_ref[...], s_ref[...], zc_ref[...], zs_ref[...], slots)
    real, imag = row.expand(pic_ref[...])
    g_ref[:, :WIDE] = row.mask * real
    g_ref[:, WIDE:] = row.mask * imag


def shifted(x, down, right):
    if down:
        x = pltpu.roll(x, (-down) % x.shape[0], 0)
    if right:
        x = pltpu.roll(x, (-right) % x.shape[1], 1)
    return x


def rounded(x):
    return x.astype(BF).astype(F32)


def refine_kernel(
    kin_ref, bin_ref, kout_ref, bout_ref, weight_ref,
    y_ref, d_ref, cot_ref, gain_ref, inside_ref,
    m0_ref, total_ref, image_ref,
    taps_ref, hidden_ref, slope_ref,
):
    inside = inside_ref[...]
    gain = gain_ref[...]

    def spread_taps(planes, sign):
        for channel in (0, 1):
            for b in range(3):
                moved = shifted(planes[channel], 0, sign * (b - 1))
                for a in range(3):
                    taps_ref[(a * 3 + b) * 2 + channel] = shifted(moved, sign * (a - 1), 0)

    def gather_taps(sign):
        planes = []
        for channel in (0, 1):
            plane = None
            for b in range(3):
                column = None
                for a in range(3):
                    piece = shifted(taps_ref[(a * 3 + b) * 2 + channel], sign * (a - 1), 0)
                    column = piece if column is None else column + piece
                column = shifted(column, 0, sign * (b - 1))
                plane = column if plane is None else plane + column
            planes.append(plane)
        return planes

    def mix(source_ref, weight_of, first):
        total = first
        for k in range(HID):
            term = weight_of(k) * source_ref[k]
            total = term if total is None else total + term
        return total

    def into_hidden(t, o, k):
        return kin_ref[((t * 9 + k // 2) * HID + o) * 2 + k % 2]

    def out_of_hidden(t, k, o):
        return kout_ref[(t * 18 + k) * HID + o]

    def refine(t, planes):
        spread_taps(planes, 1)

        @pl.loop(0, HID)
        def _(o):
            first = jnp.full(inside.shape, bin_ref[t * HID + o], F32)
            pre = mix(taps_ref, lambda k: into_hidden(t, o, k), first)
            gate = jax.nn.sigmoid(pre)
            hidden_ref[o] = inside * pre * gate
            slope_ref[t, o] = inside * gate * (1.0 + pre * (1.0 - gate))

        @pl.loop(0, HID)
        def _(k):
            taps_ref[k] = mix(hidden_ref, lambda o: out_of_hidden(t, k, o), None)

        planes = gather_taps(1)
        return [rounded(planes[i] + bout_ref[t * 2 + i]) for i in (0, 1)]

    def pull_back(t, planes):
        spread_taps(planes, -1)

        @pl.loop(0, HID)
        def _(o):
            hidden_ref[o] = slope_ref[t, o] * mix(taps_ref, lambda k: out_of_hidden(t, k, o), None)

        @pl.loop(0, HID)
        def _(k):
            channel = lax.rem(k, 2)
            base = (t * 9 + lax.div(k, 2)) * HID
            taps_ref[k] = mix(hidden_ref, lambda o: kin_ref[(base + o) * 2 + channel], None)

        return [rounded(x) for x in gather_taps(-1)]

    def planes_of(ref):
        return [ref[:, :WIDE].astype(F32), ref[:, WIDE:].astype(F32)]

    combined = planes_of(y_ref)
    m0 = refine(0, [rounded(x) for x in combined])
    for i in (0, 1):
        m0_ref[:, i * WIDE : i * WIDE + WIDE] = m0[i].astype(BF)
    state = [combined[i] + gain * m0[i] for i in (0, 1)]
    m1 = refine(1, [rounded(x) for x in state])
    for i in (0, 1):
        image_ref[:, i * WIDE : i * WIDE + WIDE] = state[i] + gain * m1[i]
    cot = planes_of(cot_ref)
    ubar1 = pull_back(1, [rounded(gain * x) for x in cot])
    normal = planes_of(d_ref)
    w0 = weight_ref[0]
    w1 = weight_ref[1]
    mbar0 = [gain * cot[i] - w1 * normal[i] + gain * ubar1[i] for i in (0, 1)]
    ubar0 = pull_back(0, [rounded(x) for x in mbar0])
    kept = w0 + (1.0 - w0)
    for i in (0, 1):
        total = (w1 + kept * (1.0 - w1)) * cot[i] + kept * ubar1[i] + ubar0[i]
        total_ref[:, i * WIDE : i * WIDE + WIDE] = total.astype(BF)


VMEM = pl.BlockSpec(memory_space=pltpu.VMEM)
SMEM = pl.BlockSpec(memory_space=pltpu.SMEM)


def padded(x):
    half = x.shape[-1] // 2
    widths = ((0, 0),) * (x.ndim - 1) + ((0, WIDE - half),)
    return jnp.concatenate([jnp.pad(x[..., :half], widths), jnp.pad(x[..., half:], widths)], axis=-1)


def unpadded(x, half):
    return jnp.concatenate([x[..., :half], x[..., WIDE : WIDE + half]], axis=-1)


def body(kspace, coil_maps, sampling, dc_weight, kernel_in, bias_in, kernel_out, bias_out, cotangent):
    coils, slots, _, width_two = kspace.shape
    rows = coil_maps.shape[2]
    half = width_two // 2
    volumes, depth, _ = sampling.shape
    coil_parts = lax.axis_size("coil")

    cosine, sine = line_tables(half)
    zcos, zsin = depth_tables(depth, volumes * coils)
    fixed = (cosine, sine, zcos, zsin)
    mask = jnp.pad(sampling.astype(F32).reshape(slots, half), ((0, 0), (0, WIDE - half)))
    maps_slice = padded(coil_maps[:, 0])
    cot_slice = padded(cotangent[0])
    k_row = padded(kspace.reshape(coils * slots, width_two))

    def to_rows(x):
        return lax.all_to_all(x, "section", split_axis=1, concat_axis=1, tiled=True)

    def sum_coils(x):
        n = coil_parts
        parts = lax.all_to_all(x.reshape(n, rows // n, x.shape[1]), "coil", 0, 0, tiled=True)
        own = jnp.sum(parts.astype(F32), axis=0).astype(BF)
        spread = jnp.broadcast_to(own[None], (n,) + own.shape)
        return lax.all_to_all(spread, "coil", 0, 0, tiled=True).reshape(x.shape)

    moved = to_rows(jnp.concatenate([maps_slice, cot_slice[None]], axis=0))
    maps_row = moved[:coils].reshape(coils * slots, 2 * WIDE)
    cot_row = moved[coils]

    out_row = jax.ShapeDtypeStruct((slots, 2 * WIDE), BF)
    y_row, d_row = pl.pallas_call(
        start_kernel,
        out_shape=(out_row, out_row),
        in_specs=[SMEM] + [VMEM] * 8,
        out_specs=(VMEM, VMEM),
        name="start",
    )(dc_weight, k_row, maps_row, cot_row, mask, *fixed)

    maps32 = maps_slice.astype(F32)
    gain = jnp.sum(maps32[..., :WIDE] ** 2 + maps32[..., WIDE:] ** 2, axis=0).astype(BF)
    moved = to_rows(jnp.stack([y_row, d_row]))
    sums = sum_coils(jnp.concatenate([moved[0], moved[1], gain], axis=1))
    sums = jnp.pad(sums, ((0, ROWPAD), (0, 0)))
    high = rows + ROWPAD
    inside = np.zeros((high, WIDE), np.float32)
    inside[:rows, :half] = 1.0

    out_slice = jax.ShapeDtypeStruct((high, 2 * WIDE), BF)
    hidden = pltpu.VMEM((HID, high, WIDE), F32)
    m0, total, image = pl.pallas_call(
        refine_kernel,
        out_shape=(out_slice, out_slice, jax.ShapeDtypeStruct((high, 2 * WIDE), F32)),
        in_specs=[SMEM] * 5 + [VMEM] * 5,
        out_specs=(VMEM,) * 3,
        scratch_shapes=[hidden, hidden, pltpu.VMEM((2, HID, high, WIDE), F32)],
        name="refine",
    )(
        kernel_in.reshape(-1), bias_in.reshape(-1), kernel_out.reshape(-1), bias_out.reshape(-1), dc_weight,
        sums[:, : 2 * WIDE], sums[:, 2 * WIDE : 4 * WIDE],
        jnp.pad(cot_slice, ((0, ROWPAD), (0, 0))), sums[:, 4 * WIDE :].astype(F32), jnp.asarray(inside),
    )

    total_row = to_rows(total[None, :rows])[0]
    grad = pl.pallas_call(
        final_kernel,
        out_shape=jax.ShapeDtypeStruct((coils * slots, 2 * WIDE), F32),
        in_specs=[VMEM] * 7,
        out_specs=VMEM,
        name="final",
    )(maps_row, total_row, mask, *fixed)

    m0_row = to_rows(m0[None, :rows])[0]
    d0_row = pl.pallas_call(
        normal_kernel,
        out_shape=out_row,
        in_specs=[VMEM] * 7,
        out_specs=VMEM,
        name="normal",
    )(maps_row, m0_row, mask, *fixed)
    d0 = sum_coils(to_rows(d0_row[None])[0]).astype(F32)
    image = image[:rows] - dc_weight[1] * d0
    return (
        unpadded(image, half)[None],
        unpadded(grad, half).reshape(coils, slots, 1, width_two),
    )


def solution(mesh):
    return jax.shard_map(
        body,
        mesh=mesh,
        in_specs=(
            P("coil", None, "section", None),
            P("coil", "section", None, None),
            P(), P(), P(), P(), P(), P(),
            P("section", None, None),
        ),
        out_specs=(P("section", None, None), P("coil", None, "section", None)),
        check_vma=False,
    )
```

time: 793 us -> 268 us (0.34)
  waiting for transfers between devices: 544 us -> 96.4 us
  blocking collectives: 0 us -> 55.9 us
  starting transfers between devices: 89.2 us -> 47 us
  matrix products: 41.8 us -> 0 us
  local copies, waits for them, and re-layouts: 56.7 us -> 19.7 us
  Pallas kernels: 0 us -> 35 us
  other arithmetic: 36.8 us -> 10.1 us
  between operations: 15.8 us -> 0.98 us
    psum x3 -> x0, waiting for transfers between devices: 410 us -> none  [combine(): lax.psum(partial_sum.astype(jnp.bfloat16), 'coil').astype(jnp.float32)]
    all_to_all x0 -> x2, blocking collectives: none -> 55.9 us  [the longest x1 31.3 us: to_rows(): return lax.all_to_all(x, 'section', split_axis=1, concat_axis=1, tiled=True)]
    dot_general x38 -> x0, matrix products: 41.8 us -> none  [the longest x4 19.3 us: conv_out(): projected = jnp.einsum('toc,cxy->toxy', kernel, hidden, precision=PRECISE)]
    all_to_all x10 -> x7, starting transfers between devices: 88.8 us -> 47 us  [the longest x4 36.1 us: to_rows(): return lax.all_to_all(x, 'section', split_axis=1, concat_axis=1, tiled=True)]
    all_to_all x10 -> x7, waiting for transfers between devices: 134 us -> 96.4 us  [the longest x4 62.4 us: to_rows(): return lax.all_to_all(x, 'section', split_axis=1, concat_axis=1, tiled=True)]
    pallas_call x0 -> x4, Pallas kernels: none -> 35 us  [the longest x1 25.5 us: body(): pl.pallas_call(refine_kernel, out_shape=(out_slice, out_slice, jax.ShapeD...]
    another operation x30 -> x1, local copies, waits for them, and re-layouts: 33.4 us -> 0.88 us  [body(): moved = to_rows(jnp.stack([y_row, d_row]))]
    another operation x10 -> x1, other arithmetic: 10 us -> 0.96 us  [body(): moved = to_rows(jnp.stack([y_row, d_row]))]
  transfers between devices with their start and end apart: 13 -> 7, of which waited for: 13 -> 7; matrix products, arithmetic and copies ran while one was open for 3% -> 4% of each run, Pallas kernels for 0% -> 1%
where the time goes in v1:
time: 268 us; the launch traced here: 265 us
  waiting for transfers between devices  96.4 us (36%)
  blocking collectives  55.9 us (21%)
  starting transfers between devices  47 us (18%)
  Pallas kernels  35 us (13%)
  local copies, waits for them, and re-layouts  19.7 us (7%)
  other arithmetic  10.1 us (4%)
    all_to_all x4, waiting for transfers between devices, to_rows(): return lax.all_to_all(x, 'section', split_axis=1, concat_axis=1, tiled=True)  62.4 us
    all_to_all x4, starting transfers between devices, to_rows(): return lax.all_to_all(x, 'section', split_axis=1, concat_axis=1, tiled=True)  36.1 us
    all_to_all x1, blocking collectives, to_rows(): return lax.all_to_all(x, 'section', split_axis=1, concat_axis=1, tiled=True)  31.3 us
    pallas_call x1, Pallas kernels, body(): pl.pallas_call(refine_kernel, out_shape=(out_slice, out_slice, jax.ShapeD...  25.5 us
    all_to_all x1, blocking collectives, sum_coils(): lax.all_to_all(x.reshape(n, rows // n, x.shape[1]), 'coil', 0, 0, tiled=T...  24.6 us
    all_to_all x2, waiting for transfers between devices, sum_coils(): return lax.all_to_all(spread, 'coil', 0, 0, tiled=True).reshape(x.shape)  24.2 us
    all_to_all x1, waiting for transfers between devices, sum_coils(): lax.all_to_all(x.reshape(n, rows // n, x.shape[1]), 'coil', 0, 0, tiled=T...  9.89 us
    all_to_all x2, starting transfers between devices, sum_coils(): return lax.all_to_all(spread, 'coil', 0, 0, tiled=True).reshape(x.shape)  7.43 us
  transfers between devices with their start and end apart: 7, of which 7 were waited for; matrix products, arithmetic and copies ran while one was open for 4% of the time, Pallas kernels for 1%

profile of v1, /device:TPU:1, one launch (start us, length us, event | category | flops | bytes accessed | tf_op | source)
XLA Modules:
  0.0 265.1 jit_solution(1825953352169692917)
XLA Ops:
  0.7 0.9 slice.100
  1.6 0.8 slice_select_fusion.1
  3.2 1.2 pad_maximum_fusion
  4.3 17.3 %all-to-all-start = ((bf16[3,64,768]{2,0,1:T(4,128)(2,1)}), bf16[3,64,768]{2,0,1:T(4,128)(2,1)S(1)}, u32[]{:S(2)}, u32[]{:S(2)}) async-start(bf16[3,64,768]{2,0,1:T(4,128)(2,1)} %pad_maximum_fusion), calls=%async_computation | async-start | bytes 786432 | tf_op jit(solution)/shard_map/all_to_all | solution.py:272
  21.8 0.8 copy-done.4
  24.0 22.0 %all-to-all-done = bf16[3,64,768]{2,0,1:T(4,128)(2,1)S(1)} async-done(((bf16[3,64,768]{2,0,1:T(4,128)(2,1)}), bf16[3,64,768]{2,0,1:T(4,128)(2,1)S(1)}, u32[]{:S(2)}, u32[]{:S(2)}) %all-to-all-start) | async-done | bytes 294944 | tf_op jit(solution)/shard_map/all_to_all | solution.py:272
  47.7 3.7 %start.1 = (bf16[64,768]{1,0:T(8,128)(2,1)}, bf16[64,768]{1,0:T(8,128)(2,1)}) custom-call(f32[2]{0:T(128)} %weight_ref.3, bf16[128,768]{1,0:T(8,128)(2,1)} %fusion.1.k_ref, bf16[128,768]{1,0:T(8,128)(2,1)} %bitcast.54, bf16[64,768]{1,0:T(8,128)(2,1)} %bitcast.69, f32[64,384]{1,0:T(8,128)} %pad.39.mask_ref, bf16[384,384]{1,0:T(8,128)(2,1)} %constant.42.c_ref, ...), custom_call_target="tpu_custom_call" | custom-call | tf_op jit(solution)/shard_map/start/pallas_call | solution.py:286
  51.4 1.0 pad_maximum_fusion.3
  52.4 0.9 copy.34
  53.3 7.3 %all-to-all-start.1 = ((bf16[2,64,768]{2,0,1:T(2,128)(2,1)}), bf16[2,64,768]{2,0,1:T(2,128)(2,1)S(1)}, u32[]{:S(2)}, u32[]{:S(2)}) async-start(bf16[2,64,768]{2,0,1:T(2,128)(2,1)} %copy.34), calls=%async_computation.1 | async-start | bytes 393216 | tf_op jit(solution)/shard_map/all_to_all | solution.py:272
  61.0 16.1 %all-to-all-done.1 = bf16[2,64,768]{2,0,1:T(2,128)(2,1)S(1)} async-done(((bf16[2,64,768]{2,0,1:T(2,128)(2,1)}), bf16[2,64,768]{2,0,1:T(2,128)(2,1)S(1)}, u32[]{:S(2)}, u32[]{:S(2)}) %all-to-all-start.1) | async-done | bytes 196640 | tf_op jit(solution)/shard_map/all_to_all | solution.py:272
  77.4 24.6 %all_to_all.45 = bf16[8,8,1920]{2,1,0:T(8,128)(2,1)S(1)} all-to-all(bf16[8,8,1920]{2,1,0:T(8,128)(2,1)S(1)} %pad_maximum_fusion.2), channel_id=1, replica_groups=mesh['section'=64,'coil'=8] {'coil'}, dimensions={0} | all-to-all | bytes 491520 | tf_op jit(solution)/shard_map/all_to_all | solution.py:276
  102.8 3.5 %all-to-all-start.3 = ((bf16[8,8,1920]{2,1,0:T(8,128)(2,1)}), bf16[8,8,1920]{2,1,0:T(8,128)(2,1)S(1)}, u32[]{:S(2)}, u32[]{:S(2)}) async-start(bf16[8,8,1920]{2,1,0:T(8,128)(2,1)} %broadcast_in_dim.28), calls=%async_computation.3 | async-start | bytes 491520 | tf_op jit(solution)/shard_map/all_to_all | solution.py:279
  109.9 11.4 %all-to-all-done.3 = bf16[8,8,1920]{2,1,0:T(8,128)(2,1)S(1)} async-done(((bf16[8,8,1920]{2,1,0:T(8,128)(2,1)}), bf16[8,8,1920]{2,1,0:T(8,128)(2,1)S(1)}, u32[]{:S(2)}, u32[]{:S(2)}) %all-to-all-start.3) | async-done | bytes 245792 | tf_op jit(solution)/shard_map/all_to_all | solution.py:279
  122.6 25.5 %refine.1 = (bf16[72,768]{1,0:T(8,128)(2,1)}, bf16[72,768]{1,0:T(8,128)(2,1)}, f32[72,768]{1,0:T(8,128)}) custom-call(f32[648]{0:T(1024)} %reshape.45.kin_ref, f32[36]{0:T(128)} %reshape.46.bin_ref, f32[648]{0:T(1024)} %reshape.47.kout_ref, f32[4]{0:T(128)} %reshape.48.bout_ref, f32[2]{0:T(128)} %weight_ref.3, bf16[72,768]{1,0:T(8,128)(2,1)} %get-tuple-element.23.y_ref, ...), custom_call_target="tpu_custom_call" | custom-call | tf_op jit(solution)/shard_map/refine/pallas_call | solution.py:305
  148.1 0.9 slice_bitcast_fusion.1
  149.8 1.2 reduce.2
  151.0 31.3 %all_to_all.46 = bf16[64,2,384]{2,1,0:T(2,128)(2,1)S(1)} all-to-all(bf16[64,2,384]{2,1,0:T(2,128)(2,1)S(1)} %reshape.54), channel_id=1, replica_groups=mesh['section'=64,'coil'=8] {'section'}, dimensions={0} | all-to-all | bytes 196608 | tf_op jit(solution)/shard_map/all_to_all | solution.py:272
  183.0 3.2 %normal.1 = bf16[64,768]{1,0:T(8,128)(2,1)} custom-call(bf16[128,768]{1,0:T(8,128)(2,1)} %bitcast.55, bf16[64,768]{1,0:T(8,128)(2,1)} %bitcast.71, f32[64,384]{1,0:T(8,128)} %pad.39.mask_ref, bf16[384,384]{1,0:T(8,128)(2,1)} %constant.42.c_ref, bf16[384,384]{1,0:T(8,128)(2,1)} %constant.43.s_ref, bf16[128,128]{1,0:T(8,128)(2,1)} %constant.44.zc_ref, ...), custom_call_target="tpu_custom_call" | custom-call | tf_op jit(solution)/shard_map/normal/pallas_call | solution.py:328
  186.2 1.0 copy.63
  187.2 1.2 reduce.3
  189.1 5.8 %all-to-all-start.5 = ((bf16[64,2,384]{2,1,0:T(2,128)(2,1)}), bf16[64,2,384]{2,1,0:T(2,128)(2,1)S(1)}, u32[]{:S(2)}, u32[]{:S(2)}) async-start(bf16[64,2,384]{2,1,0:T(2,128)(2,1)} %reshape.56), calls=%async_computation.5 | async-start | bytes 196608 | tf_op jit(solution)/shard_map/all_to_all | solution.py:272
  195.1 1.2 reduce.4
  196.9 11.5 %all-to-all-done.5 = bf16[64,2,384]{2,1,0:T(2,128)(2,1)S(1)} async-done(((bf16[64,2,384]{2,1,0:T(2,128)(2,1)}), bf16[64,2,384]{2,1,0:T(2,128)(2,1)S(1)}, u32[]{:S(2)}, u32[]{:S(2)}) %all-to-all-start.5) | async-done | bytes 98336 | tf_op jit(solution)/shard_map/all_to_all | solution.py:272
  208.4 5.7 %all-to-all-start.8 = ((bf16[64,2,384]{2,1,0:T(2,128)(2,1)}), bf16[64,2,384]{2,1,0:T(2,128)(2,1)S(1)}, u32[]{:S(2)}, u32[]{:S(2)}) async-start(bf16[64,2,384]{2,1,0:T(2,128)(2,1)} %reshape.58), calls=%async_computation.8 | async-start | bytes 196608 | tf_op jit(solution)/shard_map/all_to_all | solution.py:272
  214.9 12.8 %all-to-all-done.8 = bf16[64,2,384]{2,1,0:T(2,128)(2,1)S(1)} async-done(((bf16[64,2,384]{2,1,0:T(2,128)(2,1)}), bf16[64,2,384]{2,1,0:T(2,128)(2,1)S(1)}, u32[]{:S(2)}, u32[]{:S(2)}) %all-to-all-start.8) | async-done | bytes 98336 | tf_op jit(solution)/shard_map/all_to_all | solution.py:272
  227.7 3.5 %all-to-all-start.6 = ((bf16[8,8,768]{2,1,0:T(8,128)(2,1)}), bf16[8,8,768]{2,1,0:T(8,128)(2,1)S(1)}, u32[]{:S(2)}, u32[]{:S(2)}) async-start(bf16[8,8,768]{2,1,0:T(8,128)(2,1)} %bitcast.49), calls=%async_computation.6 | async-start | bytes 196608 | tf_op jit(solution)/shard_map/all_to_all | solution.py:276
  232.6 2.6 final.1
  235.2 9.9 %all-to-all-done.6 = bf16[8,8,768]{2,1,0:T(8,128)(2,1)S(1)} async-done(((bf16[8,8,768]{2,1,0:T(8,128)(2,1)}), bf16[8,8,768]{2,1,0:T(8,128)(2,1)S(1)}, u32[]{:S(2)}, u32[]{:S(2)}) %all-to-all-start.6) | async-done | bytes 98336 | tf_op jit(solution)/shard_map/all_to_all | solution.py:276
  245.8 3.9 %all-to-all-start.7 = ((bf16[8,8,768]{2,1,0:T(8,128)(2,1)}), bf16[8,8,768]{2,1,0:T(8,128)(2,1)S(1)}, u32[]{:S(2)}, u32[]{:S(2)}) async-start(bf16[8,8,768]{2,1,0:T(8,128)(2,1)} %broadcast_in_dim.31), calls=%async_computation.7 | async-start | bytes 196608 | tf_op jit(solution)/shard_map/all_to_all | solution.py:279
  249.8 1.1 copy.40
  250.9 12.8 %all-to-all-done.7 = bf16[8,8,768]{2,1,0:T(8,128)(2,1)S(1)} async-done(((bf16[8,8,768]{2,1,0:T(8,128)(2,1)}), bf16[8,8,768]{2,1,0:T(8,128)(2,1)S(1)}, u32[]{:S(2)}, u32[]{:S(2)}) %all-to-all-start.7) | async-done | bytes 98336 | tf_op jit(solution)/shard_map/all_to_all | solution.py:279
  (74 shorter events, 17.6 us)
Async XLA Ops:
  0.6 0.9 copy-start.8
  0.6 1.8 copy-start.3
  4.3 17.3 %copy-start.1 = (bf16[2,64,1,640]{3,1,2,0:T(8,128)(2,1)S(1)}, bf16[2,64,1,640]{3,1,2,0:T(8,128)(2,1)}, u32[]{:S(2)}) copy-start(bf16[2,64,1,640]{3,1,2,0:T(8,128)(2,1)} %param.14) | copy-start | bytes 491524
  4.3 41.7 %all-to-all-start = ((bf16[3,64,768]{2,0,1:T(4,128)(2,1)}), bf16[3,64,768]{2,0,1:T(4,128)(2,1)S(1)}, u32[]{:S(2)}, u32[]{:S(2)}) async-start(bf16[3,64,768]{2,0,1:T(4,128)(2,1)} %pad_maximum_fusion), calls=%async_computation | async-start | bytes 786432 | tf_op jit(solution)/shard_map/all_to_all | solution.py:272
  21.7 0.9 copy-start.4
  53.3 23.8 %all-to-all-start.1 = ((bf16[2,64,768]{2,0,1:T(2,128)(2,1)}), bf16[2,64,768]{2,0,1:T(2,128)(2,1)S(1)}, u32[]{:S(2)}, u32[]{:S(2)}) async-start(bf16[2,64,768]{2,0,1:T(2,128)(2,1)} %copy.34), calls=%async_computation.1 | async-start | bytes 393216 | tf_op jit(solution)/shard_map/all_to_all | solution.py:272
  102.8 3.6 %copy-start.7 = (f32[2,9,18,2]{2,3,1,0:T(2,128)S(1)}, f32[2,9,18,2]{2,3,1,0:T(2,128)}, u32[]{:S(2)}) copy-start(f32[2,9,18,2]{2,3,1,0:T(2,128)} %param.18) | copy-start | bytes 7780
  102.8 18.5 %all-to-all-start.3 = ((bf16[8,8,1920]{2,1,0:T(8,128)(2,1)}), bf16[8,8,1920]{2,1,0:T(8,128)(2,1)S(1)}, u32[]{:S(2)}, u32[]{:S(2)}) async-start(bf16[8,8,1920]{2,1,0:T(8,128)(2,1)} %broadcast_in_dim.28), calls=%async_computation.3 | async-start | bytes 491520 | tf_op jit(solution)/shard_map/all_to_all | solution.py:279
  106.6 0.7 copy-start.10
  106.6 1.3 copy-start.6
  107.9 0.7 copy-start.11
  189.1 5.8 %copy-start.5 = (bf16[72,768]{1,0:T(8,128)(2,1)S(1)}, bf16[72,768]{1,0:T(8,128)(2,1)}, u32[]{:S(2)}) copy-start(bf16[72,768]{1,0:T(8,128)(2,1)} %get-tuple-element.11) | copy-start | bytes 331780
  189.1 19.4 %all-to-all-start.5 = ((bf16[64,2,384]{2,1,0:T(2,128)(2,1)}), bf16[64,2,384]{2,1,0:T(2,128)(2,1)S(1)}, u32[]{:S(2)}, u32[]{:S(2)}) async-start(bf16[64,2,384]{2,1,0:T(2,128)(2,1)} %reshape.56), calls=%async_computation.5 | async-start | bytes 196608 | tf_op jit(solution)/shard_map/all_to_all | solution.py:272
  208.4 19.2 %all-to-all-start.8 = ((bf16[64,2,384]{2,1,0:T(2,128)(2,1)}), bf16[64,2,384]{2,1,0:T(2,128)(2,1)S(1)}, u32[]{:S(2)}, u32[]{:S(2)}) async-start(bf16[64,2,384]{2,1,0:T(2,128)(2,1)} %reshape.58), calls=%async_computation.8 | async-start | bytes 196608 | tf_op jit(solution)/shard_map/all_to_all | solution.py:272
  227.7 3.5 %copy-start.9 = (f32[2]{0:T(128)S(1)}, f32[2]{0:T(128)}, u32[]{:S(2)}) copy-start(f32[2]{0:T(128)} %weight_ref.3) | copy-start | bytes 28
  227.7 17.4 %all-to-all-start.6 = ((bf16[8,8,768]{2,1,0:T(8,128)(2,1)}), bf16[8,8,768]{2,1,0:T(8,128)(2,1)S(1)}, u32[]{:S(2)}, u32[]{:S(2)}) async-start(bf16[8,8,768]{2,1,0:T(8,128)(2,1)} %bitcast.49), calls=%async_computation.6 | async-start | bytes 196608 | tf_op jit(solution)/shard_map/all_to_all | solution.py:276
  235.2 14.5 %copy-start = (f32[128,768]{1,0:T(8,128)S(1)}, f32[128,768]{1,0:T(8,128)}, u32[]{:S(2)}) copy-start(f32[128,768]{1,0:T(8,128)} %final.1) | copy-start | bytes 1179652
  245.8 17.9 %all-to-all-start.7 = ((bf16[8,8,768]{2,1,0:T(8,128)(2,1)}), bf16[8,8,768]{2,1,0:T(8,128)(2,1)S(1)}, u32[]{:S(2)}, u32[]{:S(2)}) async-start(bf16[8,8,768]{2,1,0:T(8,128)(2,1)} %broadcast_in_dim.31), calls=%async_computation.7 | async-start | bytes 196608 | tf_op jit(solution)/shard_map/all_to_all | solution.py:279
  249.8 13.8 %copy-start.2 = (f32[72,768]{1,0:T(8,128)S(1)}, f32[72,768]{1,0:T(8,128)}, u32[]{:S(2)}) copy-start(f32[72,768]{1,0:T(8,128)} %get-tuple-element.9) | copy-start | bytes 663556

commit v2 on v1

v2 whole, which is shorter than its diff:
```python
import functools
import math

import jax
import jax.numpy as jnp
import numpy as np
from jax import lax
from jax.experimental import pallas as pl
from jax.experimental.pallas import tpu as pltpu
from jax.sharding import PartitionSpec as P

BF = jnp.bfloat16
F32 = jnp.float32
HID = 18
WIDE = 384
HALO = 8


def tables(count, wide):
    index = np.arange(count)
    angle = (index[:, None] * index[None, :] % count) * (2.0 * math.pi / count)
    cosine = np.zeros((wide, wide), np.float32)
    sine = np.zeros((wide, wide), np.float32)
    cosine[:count, :count] = np.cos(angle) / math.sqrt(count)
    sine[:count, :count] = np.sin(angle) / math.sqrt(count)
    return cosine, sine


def line_tables(count):
    cosine, sine = tables(count, WIDE)
    return jnp.asarray(cosine).astype(BF), jnp.asarray(sine).astype(BF)


def depth_tables(depth, blocks):
    cosine, sine = tables(depth, depth)
    eye = np.eye(blocks, dtype=np.float32)
    return jnp.asarray(np.kron(eye, cosine)).astype(BF), jnp.asarray(np.kron(eye, sine)).astype(BF)


def dot(a, b):
    return jnp.dot(a, b, preferred_element_type=F32)


def line_transform(real, imag, cosine, sine, sign):
    rows = real.shape[0]
    both = jnp.concatenate([real, imag], axis=0).astype(BF)
    straight = dot(both, cosine)
    crossed = dot(both, sine)
    return straight[:rows] - sign * crossed[rows:], straight[rows:] + sign * crossed[:rows]


def depth_transform(real, imag, cosine, sine, sign):
    both = jnp.concatenate([real, imag], axis=1).astype(BF)
    straight = dot(cosine, both)
    crossed = dot(sine, both)
    return (
        straight[:, :WIDE] - sign * crossed[:, WIDE:],
        straight[:, WIDE:] + sign * crossed[:, :WIDE],
    )


class Row:
    def __init__(self, mask, line, depth):
        self.mask = mask
        self.line = line
        self.depth = depth

    def take_maps(self, planes):
        self.coils = planes.shape[0] // 2
        self.maps_real = jnp.concatenate([planes[2 * i] for i in range(self.coils)], axis=0)
        self.maps_imag = jnp.concatenate([planes[2 * i + 1] for i in range(self.coils)], axis=0)

    def expand(self, picture):
        real = jnp.concatenate([picture[0]] * self.coils, axis=0)
        imag = jnp.concatenate([picture[1]] * self.coils, axis=0)
        out = (
            self.maps_real * real - self.maps_imag * imag,
            self.maps_real * imag + self.maps_imag * real,
        )
        out = line_transform(*out, *self.line, -1.0)
        return depth_transform(*out, *self.depth, -1.0)

    def inverse(self, real, imag):
        real, imag = depth_transform(real, imag, *self.depth, 1.0)
        return line_transform(real, imag, *self.line, 1.0)

    def collect(self, real, imag):
        out_real = self.maps_real * real + self.maps_imag * imag
        out_imag = self.maps_real * imag - self.maps_imag * real
        n = out_real.shape[0] // self.coils
        return [
            sum(out[i * n : i * n + n] for i in range(self.coils)) for out in (out_real, out_imag)
        ]

    def normal(self, picture):
        real, imag = self.expand(picture)
        return self.collect(*self.inverse(self.mask * real, self.mask * imag))


def shifted(x, down, right):
    if down:
        x = pltpu.roll(x, (-down) % x.shape[0], 0)
    if right:
        x = pltpu.roll(x, (-right) % x.shape[1], 1)
    return x


def rounded(x):
    return x.astype(BF).astype(F32)


class Refiner:
    def __init__(self, kin_ref, bin_ref, kout_ref, bout_ref, inside, taps_ref, hidden_ref, slope_ref):
        self.kin, self.bin, self.kout, self.bout = kin_ref, bin_ref, kout_ref, bout_ref
        self.inside = inside
        self.taps, self.hidden, self.slope = taps_ref, hidden_ref, slope_ref

    def spread_taps(self, planes, sign):
        for channel in (0, 1):
            for b in range(3):
                moved = shifted(planes[channel], 0, sign * (b - 1))
                for a in range(3):
                    self.taps[(a * 3 + b) * 2 + channel] = shifted(moved, sign * (a - 1), 0)

    def gather_taps(self, sign):
        planes = []
        for channel in (0, 1):
            plane = None
            for b in range(3):
                column = None
                for a in range(3):
                    piece = shifted(self.taps[(a * 3 + b) * 2 + channel], sign * (a - 1), 0)
                    column = piece if column is None else column + piece
                column = shifted(column, 0, sign * (b - 1))
                plane = column if plane is None else plane + column
            planes.append(plane)
        return planes

    @staticmethod
    def mix(source_ref, weight_of, first):
        total = first
        for k in range(HID):
            term = weight_of(k) * source_ref[k]
            total = term if total is None else total + term
        return total

    def into_hidden(self, t, o, k):
        return self.kin[((t * 9 + k // 2) * HID + o) * 2 + k % 2]

    def out_of_hidden(self, t, k, o):
        return self.kout[(t * 18 + k) * HID + o]

    def refine(self, t, planes):
        self.spread_taps(planes, 1)

        @pl.loop(0, HID)
        def _(o):
            first = jnp.full(self.inside.shape, self.bin[t * HID + o], F32)
            pre = self.mix(self.taps, lambda k: self.into_hidden(t, o, k), first)
            gate = jax.nn.sigmoid(pre)
            self.hidden[o] = self.inside * pre * gate
            self.slope[t, o] = self.inside * gate * (1.0 + pre * (1.0 - gate))

        @pl.loop(0, HID)
        def _(k):
            self.taps[k] = self.mix(self.hidden, lambda o: self.out_of_hidden(t, k, o), None)

        planes = self.gather_taps(1)
        return [rounded(planes[i] + self.bout[t * 2 + i]) for i in (0, 1)]

    def pull_back(self, t, planes):
        self.spread_taps(planes, -1)

        @pl.loop(0, HID)
        def _(o):
            self.hidden[o] = self.slope[t, o] * self.mix(
                self.taps, lambda k: self.out_of_hidden(t, k, o), None
            )

        @pl.loop(0, HID)
        def _(k):
            channel = lax.rem(k, 2)
            base = (t * 9 + lax.div(k, 2)) * HID
            self.taps[k] = self.mix(self.hidden, lambda o: self.kin[(base + o) * 2 + channel], None)

        return [rounded(x) for x in self.gather_taps(-1)]


def clear(first_ref, second_ref, side):
    first_ref[side] = jnp.zeros(first_ref.shape[1:], first_ref.dtype)
    second_ref[side] = jnp.zeros(second_ref.shape[1:], second_ref.dtype)


def cascade_kernel(
    parts, coil_parts,
    kin_ref, bin_ref, kout_ref, bout_ref, weight_ref,
    k_ref, maps_ref, cot_ref, gain_ref, window_ref, inside_ref, mask_ref,
    c_ref, s_ref, zc_ref, zs_ref,
    image_ref, grad_ref,
    maps_row, cot_row, gain_all,
    y_src, y_dst, d_src, d_dst, e_src, e_dst,
    edge_src, edge_dst, edge2_src, edge2_dst, win,
    m_src, m_dst, t_src, t_dst, image_src, image_dst, state_ref, ubar_ref,
    taps_ref, hidden_ref, slope_ref,
    send, recv, edge_send, edge_recv,
):
    rows = maps_ref.shape[0]
    columns = coil_parts // 2
    block = rows // columns
    me_s = lax.axis_index("section")
    me_c = lax.axis_index("coil")
    me_x = lax.rem(me_c, columns)
    me_hi = lax.div(me_c, columns)
    my_block = lax.div(me_s, block)
    active = me_hi == lax.rem(me_s, 2)
    to_self = jnp.logical_and(active, me_x == my_block)

    def holder(slot, x):
        return lax.rem(slot, 2) * columns + x

    def whenever(condition, yes, no=None):
        pl.when(condition)(yes)
        if no is not None:
            pl.when(jnp.logical_not(condition))(no)

    def push(index, src, dst, section, coil):
        mine = jnp.logical_and(section == me_s, coil == me_c)

        def near():
            pltpu.make_async_copy(src, dst, recv.at[index]).start()

        def far():
            pltpu.make_async_remote_copy(
                src, dst, send.at[index], recv.at[index],
                device_id={"section": section, "coil": coil}, device_id_type=pl.DeviceIdType.MESH,
            ).start()

        whenever(mine, near, far)

    def arrived(index, ref):
        pltpu.make_async_copy(ref, ref, recv.at[index]).wait()

    def left(index, ref):
        pltpu.make_async_copy(ref, ref, send.at[index]).wait()

    barrier = pltpu.get_barrier_semaphore()

    def greet(section, coil):
        def signal():
            pl.semaphore_signal(
                barrier, 1, device_id={"section": section, "coil": coil}, device_id_type=pl.DeviceIdType.MESH
            )

        mine = jnp.logical_and(section == me_s, coil == me_c)
        pl.when(jnp.logical_not(mine))(signal)

    @pl.loop(0, parts)
    def _(p):
        greet(p, me_c)
        greet(p, holder(p, my_block))

    @pl.loop(0, columns)
    def _(x):
        greet(me_s, holder(me_s, x))

    @pl.when(active)
    def _():
        @pl.loop(0, block)
        def _(i):
            @pl.loop(0, coil_parts)
            def _(q):
                greet(me_x * block + i, q)

        @pl.loop(0, coil_parts)
        def _(q):
            greet(me_s, q)

        pl.when(me_x > 0)(lambda: greet(me_s, me_c - 1))
        pl.when(me_x < columns - 1)(lambda: greet(me_s, me_c + 1))

    one = jnp.int32(1)
    zero = jnp.int32(0)
    act = jnp.where(active, one, zero)
    own = jnp.where(to_self, one, zero)
    sides = jnp.where(me_x > 0, one, zero) + jnp.where(me_x < columns - 1, one, zero)
    expected = (
        (parts - 1) + (parts - own) + (columns - act)
        + act * (block * coil_parts - own + (coil_parts - 1) + sides)
    )
    pl.semaphore_wait(barrier, expected)

    @pl.loop(0, parts)
    def _(k):
        p = lax.rem(me_s + k, parts)
        push(0, maps_ref.at[p], maps_row.at[me_s], p, me_c)

    @pl.loop(0, columns)
    def _(x):
        push(1, gain_ref.at[x], gain_all.at[me_c], me_s, holder(me_s, x))

    @pl.loop(0, parts)
    def _(k):
        p = lax.rem(me_s + k, parts)
        push(2, cot_ref.at[p], cot_row.at[me_s], p, me_c)

    pl.when(me_x == 0)(lambda: clear(edge_dst, edge2_dst, 0))
    pl.when(me_x == columns - 1)(lambda: clear(edge_dst, edge2_dst, 1))

    def to_holders(index, src, dst):
        place = me_c * block + lax.rem(me_s, block)

        @pl.loop(0, parts)
        def _(k):
            p = lax.rem(me_s + k, parts)
            push(index, src.at[p], dst.at[place], p, holder(p, my_block))

    def to_owners(index, src, dst):
        @pl.loop(0, block)
        def _(i):
            @pl.loop(0, coil_parts)
            def _(q):
                push(index, src.at[i], dst.at[me_s], me_x * block + i, q)

    def slots_of(ref):
        return jnp.swapaxes(ref[...].astype(F32), 0, 1)

    def summed(ref):
        all_parts = ref[...].astype(F32)
        total = all_parts[:block]
        for q in range(1, coil_parts):
            total = total + all_parts[q * block : q * block + block]
        return jnp.swapaxes(total, 0, 1)

    mask = mask_ref[...]
    coils = k_ref.shape[0] // mask.shape[0]
    row = Row(
        jnp.concatenate([mask] * coils, axis=0),
        (c_ref[...], s_ref[...]), (zc_ref[...], zs_ref[...]),
    )
    weighted = weight_ref[0] * row.mask
    start = []
    for part in (0, 1):
        measured = row.mask * k_ref[:, part * WIDE : part * WIDE + WIDE].astype(F32)
        start.append(measured - weighted * (measured - measured))
    images = row.inverse(*start)
    arrived(0, maps_row)
    row.take_maps(slots_of(maps_row))
    y_src[...] = jnp.stack(row.collect(*images), axis=1).astype(BF)
    to_holders(3, y_src, y_dst)
    arrived(2, cot_row)
    d_src[...] = jnp.stack(row.normal(slots_of(cot_row)), axis=1).astype(BF)
    to_holders(4, d_src, d_dst)

    def exchange_edges(which, src, dst, count):
        def link(side, coil):
            return pltpu.make_async_remote_copy(
                src.at[side], dst.at[1 - side],
                edge_send.at[which * 2 + side], edge_recv.at[which * 2 + 1 - side],
                device_id={"section": me_s, "coil": coil}, device_id_type=pl.DeviceIdType.MESH,
            )

        def coming(side):
            pltpu.make_async_copy(dst.at[side], dst.at[side], edge_recv.at[which * 2 + side]).wait()

        pl.when(me_x > 0)(lambda: link(0, me_c - 1).start())
        pl.when(me_x < columns - 1)(lambda: link(1, me_c + 1).start())
        pl.when(me_x > 0)(lambda: coming(0))
        pl.when(me_x < columns - 1)(lambda: coming(1))

    def open_window(first, planes, which, src, dst):
        for i, plane in enumerate(planes):
            plane = rounded(plane)
            win[first + i, HALO : HALO + block] = plane
            src[0, i] = plane[:HALO].astype(BF)
            src[1, i] = plane[block - HALO :].astype(BF)
        exchange_edges(which, src, dst, len(planes))
        for i in range(len(planes)):
            win[first + i, :HALO] = dst[0, i].astype(F32)
            win[first + i, HALO + block :] = dst[1, i].astype(F32)

    inner = slice(HALO, HALO + block)

    @pl.when(active)
    def _():
        net = Refiner(
            kin_ref, bin_ref, kout_ref, bout_ref, inside_ref[...], taps_ref, hidden_ref, slope_ref
        )
        arrived(1, gain_all)
        gains = jnp.sum(gain_all[...].astype(F32), axis=0)
        arrived(3, y_dst)
        total = summed(y_dst)
        open_window(0, [total[0], total[1], gains], 0, edge_src, edge_dst)
        gain = win[2]
        m0 = net.refine(0, [rounded(win[0]), rounded(win[1])])
        m_src[...] = jnp.stack([m0[0][inner], m0[1][inner]], axis=1).astype(BF)
        to_owners(5, m_src, m_dst)
        for i in (0, 1):
            state_ref[i] = win[i] + gain * m0[i]
        m1 = net.refine(1, [rounded(state_ref[0]), rounded(state_ref[1])])
        for i in (0, 1):
            state_ref[i] = state_ref[i] + gain * m1[i]
        ubar1 = net.pull_back(1, [rounded(gain * window_ref[i].astype(F32)) for i in (0, 1)])
        for i in (0, 1):
            ubar_ref[i] = ubar1[i]
        arrived(4, d_dst)
        total = summed(d_dst)
        open_window(3, [total[0], total[1]], 1, edge2_src, edge2_dst)
        w0 = weight_ref[0]
        w1 = weight_ref[1]
        mbar0 = [
            rounded(gain * window_ref[i].astype(F32) - w1 * win[3 + i] + gain * ubar_ref[i]) for i in (0, 1)
        ]
        ubar0 = net.pull_back(0, mbar0)
        kept = w0 + (1.0 - w0)
        out = [
            (w1 + kept * (1.0 - w1)) * window_ref[i].astype(F32) + kept * ubar_ref[i] + ubar0[i]
            for i in (0, 1)
        ]
        t_src[...] = jnp.stack([out[0][inner], out[1][inner]], axis=1).astype(BF)
        to_owners(6, t_src, t_dst)

    arrived(5, m_dst)
    e_src[...] = jnp.stack(row.normal(slots_of(m_dst)), axis=1).astype(BF)
    to_holders(7, e_src, e_dst)
    arrived(6, t_dst)
    real, imag = row.expand(slots_of(t_dst))
    grad_ref[:, :WIDE] = row.mask * real
    grad_ref[:, WIDE:] = row.mask * imag

    @pl.when(active)
    def _():
        arrived(7, e_dst)
        total = summed(e_dst)
        for i in (0, 1):
            image_src[0, i] = (state_ref[i, inner] - weight_ref[1] * total[i]).astype(BF)

        @pl.loop(0, coil_parts)
        def _(q):
            push(8, image_src.at[0], image_dst.at[me_x], me_s, q)

    arrived(8, image_dst)
    for x in range(columns):
        for i in (0, 1):
            image_ref[i, x * block : x * block + block] = image_dst[x, i].astype(F32)

    left(0, maps_ref.at[pl.ds(0, parts - 1)])
    left(2, cot_ref.at[pl.ds(0, parts - 1)])
    if columns > 1:
        whenever(active, lambda: left(1, gain_ref.at[pl.ds(0, columns - 1)]), lambda: left(1, gain_ref))
    else:
        pl.when(jnp.logical_not(active))(lambda: left(1, gain_ref))
    for index, src in ((3, y_src), (4, d_src), (7, e_src)):
        whenever(
            to_self,
            functools.partial(left, index, src.at[pl.ds(0, parts - 1)]),
            functools.partial(left, index, src),
        )

    @pl.when(active)
    def _():
        for index, like in ((5, e_dst), (6, e_dst)):
            whenever(
                to_self,
                functools.partial(left, index, like.at[pl.ds(0, block * coil_parts - 1)]),
                functools.partial(left, index, like),
            )
        left(8, image_src)
        for which, src in ((0, edge_src), (1, edge2_src)):
            for side, there in ((0, me_x > 0), (1, me_x < columns - 1)):
                def gone(which=which, side=side, src=src):
                    pltpu.make_async_copy(
                        src.at[side], src.at[side], edge_send.at[which * 2 + side]
                    ).wait()

                pl.when(there)(gone)


VMEM = pl.BlockSpec(memory_space=pltpu.VMEM)
SMEM = pl.BlockSpec(memory_space=pltpu.SMEM)


def planes_last(x):
    half = x.shape[-1] // 2
    x = x.reshape(x.shape[:-1] + (2, half))
    return jnp.pad(x, ((0, 0),) * (x.ndim - 1) + ((0, WIDE - half),))


def body(kspace, coil_maps, sampling, dc_weight, kernel_in, bias_in, kernel_out, bias_out, cotangent):
    coils, slots, _, width_two = kspace.shape
    rows = coil_maps.shape[2]
    half = width_two // 2
    volumes, depth, _ = sampling.shape
    coil_parts = lax.axis_size("coil")
    parts = lax.axis_size("section")
    columns = coil_parts // 2
    block = rows // columns
    high = block + 2 * HALO
    me_x = lax.rem(lax.axis_index("coil"), columns)

    cosine, sine = line_tables(half)
    zcos, zsin = depth_tables(depth, volumes * coils)
    mask = jnp.pad(sampling.astype(F32).reshape(slots, half), ((0, 0), (0, WIDE - half)))
    k_row = planes_last(kspace.reshape(coils * slots, width_two)).reshape(coils * slots, 2 * WIDE)
    maps_out = planes_last(jnp.swapaxes(coil_maps[:, 0], 0, 1)).reshape(rows, 2 * coils, WIDE)
    cot_out = planes_last(cotangent[0])
    gain = jnp.sum(maps_out.astype(F32) ** 2, axis=1).astype(BF).reshape(columns, block, WIDE)
    first = me_x * block
    window = lax.dynamic_slice_in_dim(
        jnp.pad(jnp.swapaxes(cot_out, 0, 1), ((0, 0), (HALO, HALO), (0, 0))), first, high, axis=1
    )
    place = first - HALO + lax.broadcasted_iota(jnp.int32, (high, WIDE), 0)
    line = lax.broadcasted_iota(jnp.int32, (high, WIDE), 1)
    inside = ((place >= 0) & (place < rows) & (line < half)).astype(F32)

    pair = pltpu.VMEM((slots, 2, WIDE), BF)
    gathered = pltpu.VMEM((coil_parts * block, 2, WIDE), BF)
    owned = pltpu.VMEM((block, 2, WIDE), BF)
    plane2 = pltpu.VMEM((2, high, WIDE), F32)
    hidden = pltpu.VMEM((HID, high, WIDE), F32)
    image, grad = pl.pallas_call(
        functools.partial(cascade_kernel, parts, coil_parts),
        out_shape=(
            jax.ShapeDtypeStruct((2, rows, WIDE), F32),
            jax.ShapeDtypeStruct((coils * slots, 2 * WIDE), F32),
        ),
        in_specs=[SMEM] * 5 + [VMEM] * 11,
        out_specs=(VMEM, VMEM),
        scratch_shapes=[
            pltpu.VMEM((slots, 2 * coils, WIDE), BF),
            pair,
            pltpu.VMEM((coil_parts, block, WIDE), BF),
            pair, gathered, pair, gathered, pair, gathered,
            pltpu.VMEM((2, 3, HALO, WIDE), BF), pltpu.VMEM((2, 3, HALO, WIDE), BF),
            pltpu.VMEM((2, 2, HALO, WIDE), BF), pltpu.VMEM((2, 2, HALO, WIDE), BF),
            pltpu.VMEM((5, high, WIDE), F32),
            owned, pair, owned, pair,
            pltpu.VMEM((coil_parts - 1, 2, block, WIDE), BF),
            pltpu.VMEM((columns, 2, block, WIDE), BF),
            plane2, plane2,
            hidden, hidden, pltpu.VMEM((2, HID, high, WIDE), F32),
            pltpu.SemaphoreType.DMA((9,)), pltpu.SemaphoreType.DMA((9,)),
            pltpu.SemaphoreType.DMA((4,)), pltpu.SemaphoreType.DMA((4,)),
        ],
        compiler_params=pltpu.CompilerParams(collective_id=0, has_side_effects=True),
        name="cascade",
    )(
        kernel_in.reshape(-1), bias_in.reshape(-1), kernel_out.reshape(-1), bias_out.reshape(-1), dc_weight,
        k_row, maps_out, cot_out, gain, window, inside, mask, cosine, sine, zcos, zsin,
    )
    image = jnp.concatenate([image[0, :, :half], image[1, :, :half]], axis=-1)
    grad = jnp.concatenate([grad[:, :half], grad[:, WIDE : WIDE + half]], axis=-1)
    return image[None], grad.reshape(coils, slots, 1, width_two)


def solution(mesh):
    return jax.shard_map(
        body,
        mesh=mesh,
        in_specs=(
            P("coil", None, "section", None),
            P("coil", "section", None, None),
            P(), P(), P(), P(), P(), P(),
            P("section", None, None),
        ),
        out_specs=(P("section", None, None), P("coil", None, "section", None)),
        check_vma=False,
    )
```

time: 268 us -> 111 us (0.41)
  waiting for transfers between devices: 96.4 us -> 0 us
  Pallas kernels: 35 us -> 95 us
  blocking collectives: 55.9 us -> 0 us
  starting transfers between devices: 47 us -> 0 us
  local copies, waits for them, and re-layouts: 19.7 us -> 12.2 us
  other arithmetic: 10.1 us -> 2.66 us
    all_to_all x7 -> x0, waiting for transfers between devices: 96.4 us -> none  [the longest x4 62.4 us: to_rows(): return lax.all_to_all(x, 'section', split_axis=1, concat_axis=1, tiled=True)]
    pallas_call x4 -> x1, Pallas kernels: 35 us -> 95 us  [body(): pl.pallas_call(functools.partial(cascade_kernel, parts, coil_parts), out_...]
    all_to_all x2 -> x0, blocking collectives: 55.9 us -> none  [the longest x1 31.3 us: to_rows(): return lax.all_to_all(x, 'section', split_axis=1, concat_axis=1, tiled=True)]
    all_to_all x7 -> x0, starting transfers between devices: 47 us -> none  [the longest x4 36.1 us: to_rows(): return lax.all_to_all(x, 'section', split_axis=1, concat_axis=1, tiled=True)]
    unnamed x38 -> x16, local copies, waits for them, and re-layouts: 7.07 us -> 2.56 us
    slice x11 -> x1, local copies, waits for them, and re-layouts: 3.91 us -> 0.03 us  [body(): grad = jnp.concatenate([grad[:, :half], grad[:, WIDE:WIDE + half]], axis=-1)]
    broadcast_in_dim x8 -> x0, local copies, waits for them, and re-layouts: 3.77 us -> none  [the longest x2 1.36 us: sum_coils(): spread = jnp.broadcast_to(own[None], (n,) + own.shape)]
    unnamed x3 -> x0, other arithmetic: 3.56 us -> none
  transfers between devices with their start and end apart: 7 -> 0, of which waited for: 7 -> 0; matrix products, arithmetic and copies ran while one was open for 4% -> 0% of each run, Pallas kernels for 1% -> 0%
where the time goes in v2:
time: 111 us
  Pallas kernels  95 us (86%)
  local copies, waits for them, and re-layouts  12.2 us (11%)
  other arithmetic  2.66 us (2%)
    pallas_call x1, Pallas kernels, body(): pl.pallas_call(functools.partial(cascade_kernel, parts, coil_parts), out_...  95 us
    unnamed x16, local copies, waits for them, and re-layouts  2.56 us

profile of v2, /device:TPU:1, one launch (start us, length us, event | category | flops | bytes accessed | tf_op | source)
XLA Modules:
  0.0 110.7 jit_solution(5861245256591879608)
XLA Ops:
  0.6 0.0 copy-start.3
  0.7 1.4 %reshape.35.bin_ref = f32[36]{0:T(128)} reshape(f32[2,18]{1,0:T(2,128)} %param.18) | data formatting | bytes 288 | tf_op jit(solution)/shard_map/reshape | solution.py:547
  2.0 1.3 %reshape.37.bout_ref = f32[4]{0:T(128)} reshape(f32[2,2]{1,0:T(2,128)} %param.20) | data formatting | bytes 32 | tf_op jit(solution)/shard_map/reshape | solution.py:547
  3.3 1.4 %reshape.36.kout_ref = f32[648]{0:T(1024)} reshape(f32[2,9,2,18]{3,2,1,0:T(2,128)} %param.19) | data formatting | bytes 5184 | tf_op jit(solution)/shard_map/reshape | solution.py:547
  4.7 0.7 and_convert_fusion.inside_ref
  5.5 0.0 copy-start.4
  5.5 0.6 pad.24.mask_ref
  6.1 0.2 copy-done.4
  6.3 0.1 reshape_squeeze.3
  6.5 0.6 pad_dynamic-slice_fusion.window_ref
  7.2 0.1 copy.24
  7.3 0.7 pad.22.clone.cot_ref
  8.0 0.1 copy-done.1
  8.1 0.2 reshape.39
  8.3 1.1 multiply_reduce_fusion
  9.4 0.1 copy.19
  9.5 0.2 pad.21
  9.7 0.0 copy-start.2
  9.7 0.8 reshape.40.maps_ref
  10.5 0.1 copy-done.2
  10.6 0.2 reshape_reshape.3
  10.8 0.2 pad.20
  11.0 0.0 copy-start.5
  11.0 0.7 copy.23
  11.7 0.0 copy-done.5
  11.7 0.2 copy.18
  11.9 0.7 reshape.34.kin_ref
  12.7 95.0 %cascade.1 = (f32[2,64,384]{2,1,0:T(8,128)}, f32[128,768]{1,0:T(8,128)}) custom-call(f32[648]{0:T(1024)} %reshape.34.kin_ref, f32[36]{0:T(128)} %reshape.35.bin_ref, f32[648]{0:T(1024)} %reshape.36.kout_ref, f32[4]{0:T(128)} %reshape.37.bout_ref, f32[2]{0:T(128)} %weight_ref.1, bf16[128,768]{1,0:T(8,128)(2,1)} %bitcast.24, ...), custom_call_target="tpu_custom_call" | custom-call | tf_op jit(solution)/shard_map/cascade/pallas_call | solution.py:520
  107.7 1.0 slice_bitcast_fusion.1
  108.7 0.8 maximum_bitcast_fusion
  109.5 0.1 pad_maximum_fusion
  109.6 1.1 copy.22
  (10 shorter events, 0.1 us)
Async XLA Ops:
  0.6 4.8 %copy-start.3 = (s32[2,32,320]{2,1,0:T(8,128)S(1)}, s32[2,32,320]{2,1,0:T(8,128)}, u32[]{:S(2)}) copy-start(s32[2,32,320]{2,1,0:T(8,128)} %param.15) | copy-start | bytes 245764
  5.5 0.9 copy-start.4
  7.2 0.9 copy-start.1
  9.7 0.9 copy-start.2
  11.0 0.7 copy-start.5
  107.7 1.8 %copy-start = (f32[128,768]{1,0:T(8,128)S(1)}, f32[128,768]{1,0:T(8,128)}, u32[]{:S(2)}) copy-start(f32[128,768]{1,0:T(8,128)} %get-tuple-element.5) | copy-start | bytes 1179652

commit v3 on v2

--- a/solution.py
+++ b/solution.py
@@ -66,9 +66,9 @@
         self.depth = depth
 
     def take_maps(self, planes):
-        self.coils = planes.shape[0] // 2
-        self.maps_real = jnp.concatenate([planes[2 * i] for i in range(self.coils)], axis=0)
-        self.maps_imag = jnp.concatenate([planes[2 * i + 1] for i in range(self.coils)], axis=0)
+        self.coils = planes.shape[0]
+        stacked = jnp.concatenate([planes[i] for i in range(self.coils)], axis=0)
+        self.maps_real, self.maps_imag = planes_of(stacked)
 
     def expand(self, picture):
         real = jnp.concatenate([picture[0]] * self.coils, axis=0)
@@ -103,6 +103,19 @@
     if right:
         x = pltpu.roll(x, (-right) % x.shape[1], 1)
     return x
+
+
+def widen(x):
+    return jnp.concatenate([x, jnp.zeros((x.shape[0], WIDE - x.shape[1]), x.dtype)], axis=1)
+
+
+def planes_of(x):
+    half = x.shape[1] // 2
+    return [widen(x[:, :half].astype(F32)), widen(x[:, half:].astype(F32))]
+
+
+def packed(planes, half):
+    return jnp.concatenate([planes[0][:, :half], planes[1][:, :half]], axis=1)
 
 
 def rounded(x):
@@ -145,17 +158,19 @@
         return total
 
     def into_hidden(self, t, o, k):
-        return self.kin[((t * 9 + k // 2) * HID + o) * 2 + k % 2]
+        return self.kin[t, k // 2, k % 2, o]
 
     def out_of_hidden(self, t, k, o):
-        return self.kout[(t * 18 + k) * HID + o]
+        if isinstance(k, int):
+            return self.kout[t, k // 2, k % 2, o]
+        return self.kout[t, lax.div(k, 2), lax.rem(k, 2), o]
 
     def refine(self, t, planes):
         self.spread_taps(planes, 1)
 
         @pl.loop(0, HID)
         def _(o):
-            first = jnp.full(self.inside.shape, self.bin[t * HID + o], F32)
+            first = jnp.full(self.inside.shape, self.bin[t, o], F32)
             pre = self.mix(self.taps, lambda k: self.into_hidden(t, o, k), first)
             gate = jax.nn.sigmoid(pre)
             self.hidden[o] = self.inside * pre * gate
@@ -166,7 +181,7 @@
             self.taps[k] = self.mix(self.hidden, lambda o: self.out_of_hidden(t, k, o), None)
 
         planes = self.gather_taps(1)
-        return [rounded(planes[i] + self.bout[t * 2 + i]) for i in (0, 1)]
+        return [rounded(planes[i] + self.bout[t, i]) for i in (0, 1)]
 
     def pull_back(self, t, planes):
         self.spread_taps(planes, -1)
@@ -179,9 +194,9 @@
 
         @pl.loop(0, HID)
         def _(k):
+            tap = lax.div(k, 2)
             channel = lax.rem(k, 2)
-            base = (t * 9 + lax.div(k, 2)) * HID
-            self.taps[k] = self.mix(self.hidden, lambda o: self.kin[(base + o) * 2 + channel], None)
+            self.taps[k] = self.mix(self.hidden, lambda o: self.kin[t, tap, channel, o], None)
 
         return [rounded(x) for x in self.gather_taps(-1)]
 
@@ -194,9 +209,10 @@
 def cascade_kernel(
     parts, coil_parts,
     kin_ref, bin_ref, kout_ref, bout_ref, weight_ref,
-    k_ref, maps_ref, cot_ref, gain_ref, window_ref, inside_ref, mask_ref,
-    c_ref, s_ref, zc_ref, zs_ref,
+    maps_any, cot_any, sampling_any, k_any, c_any, s_any, zc_any, zs_any,
     image_ref, grad_ref,
+    maps_in, cot_in, sampling_in, k_ref, c_ref, s_ref, zc_ref, zs_ref, load,
+    maps_ref, cot_ref, gain_ref, cot_pad,
     maps_row, cot_row, gain_all,
     y_src, y_dst, d_src, d_dst, e_src, e_dst,
     edge_src, edge_dst, edge2_src, edge2_dst, win,
@@ -205,6 +221,7 @@
     send, recv, edge_send, edge_recv,
 ):
     rows = maps_ref.shape[0]
+    half = sampling_in.shape[1]
     columns = coil_parts // 2
     block = rows // columns
     me_s = lax.axis_index("section")
@@ -246,48 +263,55 @@
     barrier = pltpu.get_barrier_semaphore()
 
     def greet(section, coil):
-        def signal():
-            pl.semaphore_signal(
-                barrier, 1, device_id={"section": section, "coil": coil}, device_id_type=pl.DeviceIdType.MESH
+        pl.semaphore_signal(
+            barrier, 1, device_id={"section": section, "coil": coil}, device_id_type=pl.DeviceIdType.MESH
+        )
+
+    @pl.loop(1, parts)
+    def _(k):
+        greet(lax.rem(me_s + k, parts), me_c)
+
+    @pl.loop(1, coil_parts)
+    def _(k):
+        greet(me_s, lax.rem(me_c + k, coil_parts))
+
+    loads = [
+        pltpu.make_async_copy(src, dst, load.at[i])
+        for i, (src, dst) in enumerate(
+            zip(
+                (maps_any, cot_any, sampling_any, k_any, c_any, s_any, zc_any, zs_any),
+                (maps_in, cot_in, sampling_in, k_ref, c_ref, s_ref, zc_ref, zs_ref),
             )
-
-        mine = jnp.logical_and(section == me_s, coil == me_c)
-        pl.when(jnp.logical_not(mine))(signal)
-
-    @pl.loop(0, parts)
-    def _(p):
-        greet(p, me_c)
-        greet(p, holder(p, my_block))
-
-    @pl.loop(0, columns)
-    def _(x):
-        greet(me_s, holder(me_s, x))
-
-    @pl.when(active)
-    def _():
-        @pl.loop(0, block)
-        def _(i):
-            @pl.loop(0, coil_parts)
-            def _(q):
-                greet(me_x * block + i, q)
-
-        @pl.loop(0, coil_parts)
-        def _(q):
-            greet(me_s, q)
-
-        pl.when(me_x > 0)(lambda: greet(me_s, me_c - 1))
-        pl.when(me_x < columns - 1)(lambda: greet(me_s, me_c + 1))
-
-    one = jnp.int32(1)
-    zero = jnp.int32(0)
-    act = jnp.where(active, one, zero)
-    own = jnp.where(to_self, one, zero)
-    sides = jnp.where(me_x > 0, one, zero) + jnp.where(me_x < columns - 1, one, zero)
-    expected = (
-        (parts - 1) + (parts - own) + (columns - act)
-        + act * (block * coil_parts - own + (coil_parts - 1) + sides)
-    )
-    pl.semaphore_wait(barrier, expected)
+        )
+    ]
+    for copy in loads:
+        copy.start()
+
+    loads[0].wait()
+    maps_ref[...] = jnp.swapaxes(maps_in[...], 0, 1)
+    gain = None
+    for i in range(maps_in.shape[0]):
+        for plane in planes_of(maps_in[i]):
+            gain = plane * plane if gain is None else gain + plane * plane
+    for x in range(columns):
+        gain_ref[x] = gain[x * block : x * block + block].astype(BF)
+    loads[1].wait()
+    cot_planes = planes_of(cot_in[...])
+    cot_ref[...] = jnp.stack(cot_planes, axis=1).astype(BF)
+    for i in (0, 1):
+        cot_pad[i, :HALO] = jnp.zeros((HALO, WIDE), F32)
+        cot_pad[i, HALO + rows :] = jnp.zeros((HALO, WIDE), F32)
+        cot_pad[i, HALO : HALO + rows] = cot_planes[i]
+    high = block + 2 * HALO
+    first_row = pl.multiple_of(me_x * block, HALO)
+    window = [cot_pad[i, pl.ds(first_row, high), :] for i in (0, 1)]
+    place = first_row - HALO + lax.broadcasted_iota(jnp.int32, (high, WIDE), 0)
+    line = lax.broadcasted_iota(jnp.int32, (high, WIDE), 1)
+    inside = jnp.where((place >= 0) & (place < rows) & (line < half), 1.0, 0.0).astype(F32)
+    loads[2].wait()
+    mask = widen(sampling_in[...].astype(F32))
+
+    pl.semaphore_wait(barrier, parts - 1 + coil_parts - 1)
 
     @pl.loop(0, parts)
     def _(k):
@@ -331,16 +355,17 @@
             total = total + all_parts[q * block : q * block + block]
         return jnp.swapaxes(total, 0, 1)
 
-    mask = mask_ref[...]
-    coils = k_ref.shape[0] // mask.shape[0]
+    coils = maps_in.shape[0]
+    for copy in loads[3:]:
+        copy.wait()
     row = Row(
         jnp.concatenate([mask] * coils, axis=0),
         (c_ref[...], s_ref[...]), (zc_ref[...], zs_ref[...]),
     )
     weighted = weight_ref[0] * row.mask
     start = []
-    for part in (0, 1):
-        measured = row.mask * k_ref[:, part * WIDE : part * WIDE + WIDE].astype(F32)
+    for part in planes_of(k_ref[...]):
+        measured = row.mask * part
         start.append(measured - weighted * (measured - measured))
     images = row.inverse(*start)
     arrived(0, maps_row)
@@ -383,7 +408,7 @@
     @pl.when(active)
     def _():
         net = Refiner(
-            kin_ref, bin_ref, kout_ref, bout_ref, inside_ref[...], taps_ref, hidden_ref, slope_ref
+            kin_ref, bin_ref, kout_ref, bout_ref, inside, taps_ref, hidden_ref, slope_ref
         )
         arrived(1, gain_all)
         gains = jnp.sum(gain_all[...].astype(F32), axis=0)
@@ -399,7 +424,7 @@
         m1 = net.refine(1, [rounded(state_ref[0]), rounded(state_ref[1])])
         for i in (0, 1):
             state_ref[i] = state_ref[i] + gain * m1[i]
-        ubar1 = net.pull_back(1, [rounded(gain * window_ref[i].astype(F32)) for i in (0, 1)])
+        ubar1 = net.pull_back(1, [rounded(gain * window[i]) for i in (0, 1)])
         for i in (0, 1):
             ubar_ref[i] = ubar1[i]
         arrived(4, d_dst)
@@ -408,12 +433,12 @@
         w0 = weight_ref[0]
         w1 = weight_ref[1]
         mbar0 = [
-            rounded(gain * window_ref[i].astype(F32) - w1 * win[3 + i] + gain * ubar_ref[i]) for i in (0, 1)
+            rounded(gain * window[i] - w1 * win[3 + i] + gain * ubar_ref[i]) for i in (0, 1)
         ]
         ubar0 = net.pull_back(0, mbar0)
         kept = w0 + (1.0 - w0)
         out = [
-            (w1 + kept * (1.0 - w1)) * window_ref[i].astype(F32) + kept * ubar_ref[i] + ubar0[i]
+            (w1 + kept * (1.0 - w1)) * window[i] + kept * ubar_ref[i] + ubar0[i]
             for i in (0, 1)
         ]
         t_src[...] = jnp.stack([out[0][inner], out[1][inner]], axis=1).astype(BF)
@@ -424,8 +449,7 @@
     to_holders(7, e_src, e_dst)
     arrived(6, t_dst)
     real, imag = row.expand(slots_of(t_dst))
-    grad_ref[:, :WIDE] = row.mask * real
-    grad_ref[:, WIDE:] = row.mask * imag
+    grad_ref[...] = packed([row.mask * real, row.mask * imag], half)
 
     @pl.when(active)
     def _():
@@ -440,8 +464,7 @@
 
     arrived(8, image_dst)
     for x in range(columns):
-        for i in (0, 1):
-            image_ref[i, x * block : x * block + block] = image_dst[x, i].astype(F32)
+        image_ref[x * block : x * block + block] = packed([image_dst[x, i].astype(F32) for i in (0, 1)], half)
 
     left(0, maps_ref.at[pl.ds(0, parts - 1)])
     left(2, cot_ref.at[pl.ds(0, parts - 1)])
@@ -479,12 +502,6 @@
 SMEM = pl.BlockSpec(memory_space=pltpu.SMEM)
 
 
-def planes_last(x):
-    half = x.shape[-1] // 2
-    x = x.reshape(x.shape[:-1] + (2, half))
-    return jnp.pad(x, ((0, 0),) * (x.ndim - 1) + ((0, WIDE - half),))
-
-
 def body(kspace, coil_maps, sampling, dc_weight, kernel_in, bias_in, kernel_out, bias_out, cotangent):
     coils, slots, _, width_two = kspace.shape
     rows = coil_maps.shape[2]
@@ -495,22 +512,13 @@
     columns = coil_parts // 2
     block = rows // columns
     high = block + 2 * HALO
-    me_x = lax.rem(lax.axis_index("coil"), columns)
 
     cosine, sine = line_tables(half)
     zcos, zsin = depth_tables(depth, volumes * coils)
-    mask = jnp.pad(sampling.astype(F32).reshape(slots, half), ((0, 0), (0, WIDE - half)))
-    k_row = planes_last(kspace.reshape(coils * slots, width_two)).reshape(coils * slots, 2 * WIDE)
-    maps_out = planes_last(jnp.swapaxes(coil_maps[:, 0], 0, 1)).reshape(rows, 2 * coils, WIDE)
-    cot_out = planes_last(cotangent[0])
-    gain = jnp.sum(maps_out.astype(F32) ** 2, axis=1).astype(BF).reshape(columns, block, WIDE)
-    first = me_x * block
-    window = lax.dynamic_slice_in_dim(
-        jnp.pad(jnp.swapaxes(cot_out, 0, 1), ((0, 0), (HALO, HALO), (0, 0))), first, high, axis=1
+    operands = (
+        coil_maps[:, 0], cotangent[0], sampling.reshape(slots, half), kspace.reshape(coils * slots, width_two),
+        cosine, sine, zcos, zsin,
     )
-    place = first - HALO + lax.broadcasted_iota(jnp.int32, (high, WIDE), 0)
-    line = lax.broadcasted_iota(jnp.int32, (high, WIDE), 1)
-    inside = ((place >= 0) & (place < rows) & (line < half)).astype(F32)
 
     pair = pltpu.VMEM((slots, 2, WIDE), BF)
     gathered = pltpu.VMEM((coil_parts * block, 2, WIDE), BF)
@@ -520,13 +528,19 @@
     image, grad = pl.pallas_call(
         functools.partial(cascade_kernel, parts, coil_parts),
         out_shape=(
-            jax.ShapeDtypeStruct((2, rows, WIDE), F32),
-            jax.ShapeDtypeStruct((coils * slots, 2 * WIDE), F32),
+            jax.ShapeDtypeStruct((rows, width_two), F32),
+            jax.ShapeDtypeStruct((coils * slots, width_two), F32),
         ),
-        in_specs=[SMEM] * 5 + [VMEM] * 11,
+        in_specs=[SMEM] * 5 + [pl.BlockSpec(memory_space=pl.ANY)] * 8,
         out_specs=(VMEM, VMEM),
         scratch_shapes=[
-            pltpu.VMEM((slots, 2 * coils, WIDE), BF),
+            *(pltpu.VMEM(x.shape, x.dtype) for x in operands),
+            pltpu.SemaphoreType.DMA((8,)),
+            pltpu.VMEM((rows, coils, width_two), BF),
+            pltpu.VMEM((rows, 2, WIDE), BF),
+            pltpu.VMEM((columns, block, WIDE), BF),
+            pltpu.VMEM((2, rows + 2 * HALO, WIDE), F32),
+            pltpu.VMEM((slots, coils, width_two), BF),
             pair,
             pltpu.VMEM((coil_parts, block, WIDE), BF),
             pair, gathered, pair, gathered, pair, gathered,
@@ -544,11 +558,8 @@
         compiler_params=pltpu.CompilerParams(collective_id=0, has_side_effects=True),
         name="cascade",
     )(
-        kernel_in.reshape(-1), bias_in.reshape(-1), kernel_out.reshape(-1), bias_out.reshape(-1), dc_weight,
-        k_row, maps_out, cot_out, gain, window, inside, mask, cosine, sine, zcos, zsin,
+        jnp.swapaxes(kernel_in, 2, 3), bias_in, kernel_out, bias_out, dc_weight, *operands,
     )
-    image = jnp.concatenate([image[0, :, :half], image[1, :, :half]], axis=-1)
-    grad = jnp.concatenate([grad[:, :half], grad[:, WIDE : WIDE + half]], axis=-1)
     return image[None], grad.reshape(coils, slots, 1, width_two)
 
 

time: 111 us -> 95.3 us (0.86)
  local copies, waits for them, and re-layouts: 12.2 us -> 2.74 us
  Pallas kernels: 95 us -> 91.6 us
  other arithmetic: 2.66 us -> 0 us
    reshape x7 -> x0, local copies, waits for them, and re-layouts: 5.91 us -> none  [the longest x1 1.43 us: body(): kernel_out.reshape(-1)]
    pallas_call x1, Pallas kernels: 95 us -> 91.6 us  [body(): pl.pallas_call(functools.partial(cascade_kernel, parts, coil_parts), out_...]
    pad x4 -> x0, local copies, waits for them, and re-layouts: 1.73 us -> none  [the longest x3 1.08 us: planes_last(): return jnp.pad(x, ((0, 0),) * (x.ndim - 1) + ((0, WIDE - half),))]
    unnamed x16 -> x4, local copies, waits for them, and re-layouts: 2.56 us -> 2.74 us
where the time goes in v3:
time: 95.3 us; the launch traced here: 95 us
  Pallas kernels  91.6 us (96%)
  local copies, waits for them, and re-layouts  2.74 us (3%)
    pallas_call x1, Pallas kernels, body(): pl.pallas_call(functools.partial(cascade_kernel, parts, coil_parts), out_...  91.6 us
    unnamed x4, local copies, waits for them, and re-layouts  2.74 us

profile of v3, /device:TPU:1, one launch (start us, length us, event | category | flops | bytes accessed | tf_op | source)
XLA Modules:
  0.0 95.0 jit_solution(10759961336421422711)
XLA Ops:
  0.6 91.6 %cascade.1 = (f32[64,640]{1,0:T(8,128)}, f32[128,640]{1,0:T(8,128)}) custom-call(f32[2,9,2,18]{3,2,1,0:T(2,128)} %bitcast.13, f32[2,18]{1,0:T(2,128)} %bin_ref.1, f32[2,9,2,18]{3,2,1,0:T(2,128)} %kout_ref.1, f32[2,2]{1,0:T(2,128)} %bout_ref.1, f32[2]{0:T(128)} %weight_ref.1, bf16[2,64,640]{2,1,0:T(8,128)(2,1)} %bitcast.9, bf16[64,640]{1,0:T(8,128)(2,1)} %bitcast.12, ...), custom_call_target="tpu_custom_call" | custom-call | tf_op jit(solution)/shard_map/cascade/pallas_call | solution.py:528
  92.3 0.0 copy-start
  92.3 2.1 %copy.15 = f32[2,64,1,640]{3,2,1,0:T(1,128)} copy(f32[2,64,1,640]{3,1,0,2:T(8,128)} %bitcast.7) | data formatting | bytes 655360
  94.3 0.0 copy-done
  94.3 0.7 copy.17
Async XLA Ops:
  92.3 2.1 %copy-start = (f32[64,640]{1,0:T(8,128)S(1)}, f32[64,640]{1,0:T(8,128)}, u32[]{:S(2)}) copy-start(f32[64,640]{1,0:T(8,128)} %get-tuple-element.4) | copy-start | bytes 491524

commit v4 on v3

--- a/solution.py
+++ b/solution.py
@@ -216,7 +216,7 @@
     maps_row, cot_row, gain_all,
     y_src, y_dst, d_src, d_dst, e_src, e_dst,
     edge_src, edge_dst, edge2_src, edge2_dst, win,
-    m_src, m_dst, t_src, t_dst, image_src, image_dst, state_ref, ubar_ref,
+    m_src, m_dst, t_src, t_dst, image_src, image_dst, twin_src, twin_dst, state_ref, ubar_ref,
     taps_ref, hidden_ref, slope_ref,
     send, recv, edge_send, edge_recv,
 ):
@@ -240,19 +240,22 @@
         if no is not None:
             pl.when(jnp.logical_not(condition))(no)
 
+    def near(index, src, dst):
+        pltpu.make_async_copy(src, dst, recv.at[index]).start()
+
+    def far(index, src, dst, section, coil):
+        pltpu.make_async_remote_copy(
+            src, dst, send.at[index], recv.at[index],
+            device_id={"section": section, "coil": coil}, device_id_type=pl.DeviceIdType.MESH,
+        ).start()
+
     def push(index, src, dst, section, coil):
         mine = jnp.logical_and(section == me_s, coil == me_c)
-
-        def near():
-            pltpu.make_async_copy(src, dst, recv.at[index]).start()
-
-        def far():
-            pltpu.make_async_remote_copy(
-                src, dst, send.at[index], recv.at[index],
-                device_id={"section": section, "coil": coil}, device_id_type=pl.DeviceIdType.MESH,
-            ).start()
-
-        whenever(mine, near, far)
+        whenever(
+            mine,
+            lambda: near(index, src, dst),
+            lambda: far(index, src, dst, section, coil),
+        )
 
     def arrived(index, ref):
         pltpu.make_async_copy(ref, ref, recv.at[index]).wait()
@@ -313,37 +316,51 @@
 
     pl.semaphore_wait(barrier, parts - 1 + coil_parts - 1)
 
-    @pl.loop(0, parts)
-    def _(k):
-        p = lax.rem(me_s + k, parts)
-        push(0, maps_ref.at[p], maps_row.at[me_s], p, me_c)
+    def to_section(index, src, dst):
+        near(index, src.at[me_s], dst.at[me_s])
+
+        @pl.loop(1, parts)
+        def _(k):
+            p = lax.rem(me_s + k, parts)
+            far(index, src.at[p], dst.at[me_s], p, me_c)
+
+    to_section(0, maps_ref, maps_row)
 
     @pl.loop(0, columns)
     def _(x):
         push(1, gain_ref.at[x], gain_all.at[me_c], me_s, holder(me_s, x))
 
-    @pl.loop(0, parts)
-    def _(k):
-        p = lax.rem(me_s + k, parts)
-        push(2, cot_ref.at[p], cot_row.at[me_s], p, me_c)
-
     pl.when(me_x == 0)(lambda: clear(edge_dst, edge2_dst, 0))
     pl.when(me_x == columns - 1)(lambda: clear(edge_dst, edge2_dst, 1))
 
+    spot = me_c * block + lax.rem(me_s, block)
+
     def to_holders(index, src, dst):
-        place = me_c * block + lax.rem(me_s, block)
-
-        @pl.loop(0, parts)
+        push(index, src.at[me_s], dst.at[spot], me_s, holder(me_s, my_block))
+
+        @pl.loop(1, parts)
         def _(k):
             p = lax.rem(me_s + k, parts)
-            push(index, src.at[p], dst.at[place], p, holder(p, my_block))
+            far(index, src.at[p], dst.at[spot], p, holder(p, my_block))
+
+    def to_both_holders(index, src, dst):
+        for hi in (0, 1):
+            push(index, src.at[me_s], dst.at[spot], me_s, hi * columns + my_block)
+
+        @pl.loop(1, parts)
+        def _(k):
+            p = lax.rem(me_s + k, parts)
+            for hi in (0, 1):
+                far(index, src.at[p], dst.at[spot], p, hi * columns + my_block)
 
     def to_owners(index, src, dst):
         @pl.loop(0, block)
         def _(i):
-            @pl.loop(0, coil_parts)
-            def _(q):
-                push(index, src.at[i], dst.at[me_s], me_x * block + i, q)
+            push(index, src.at[i], dst.at[me_s], me_x * block + i, me_c)
+
+            @pl.loop(1, coil_parts)
+            def _(k):
+                far(index, src.at[i], dst.at[me_s], me_x * block + i, lax.rem(me_c + k, coil_parts))
 
     def slots_of(ref):
         return jnp.swapaxes(ref[...].astype(F32), 0, 1)
@@ -372,9 +389,7 @@
     row.take_maps(slots_of(maps_row))
     y_src[...] = jnp.stack(row.collect(*images), axis=1).astype(BF)
     to_holders(3, y_src, y_dst)
-    arrived(2, cot_row)
-    d_src[...] = jnp.stack(row.normal(slots_of(cot_row)), axis=1).astype(BF)
-    to_holders(4, d_src, d_dst)
+    to_section(2, cot_ref, cot_row)
 
     def exchange_edges(which, src, dst, count):
         def link(side, coil):
@@ -405,28 +420,45 @@
 
     inner = slice(HALO, HALO + block)
 
+    net = Refiner(kin_ref, bin_ref, kout_ref, bout_ref, inside, taps_ref, hidden_ref, slope_ref)
+
     @pl.when(active)
     def _():
-        net = Refiner(
-            kin_ref, bin_ref, kout_ref, bout_ref, inside, taps_ref, hidden_ref, slope_ref
-        )
         arrived(1, gain_all)
         gains = jnp.sum(gain_all[...].astype(F32), axis=0)
         arrived(3, y_dst)
         total = summed(y_dst)
         open_window(0, [total[0], total[1], gains], 0, edge_src, edge_dst)
-        gain = win[2]
         m0 = net.refine(0, [rounded(win[0]), rounded(win[1])])
         m_src[...] = jnp.stack([m0[0][inner], m0[1][inner]], axis=1).astype(BF)
         to_owners(5, m_src, m_dst)
         for i in (0, 1):
-            state_ref[i] = win[i] + gain * m0[i]
+            state_ref[i] = win[i] + win[2] * m0[i]
+
+    arrived(2, cot_row)
+    d_src[...] = jnp.stack(row.normal(slots_of(cot_row)), axis=1).astype(BF)
+    to_holders(4, d_src, d_dst)
+
+    twin = (1 - me_hi) * columns + me_x
+
+    @pl.when(active)
+    def _():
+        gain = win[2]
         m1 = net.refine(1, [rounded(state_ref[0]), rounded(state_ref[1])])
         for i in (0, 1):
-            state_ref[i] = state_ref[i] + gain * m1[i]
+            twin_src[i] = (state_ref[i] + gain * m1[i])[inner]
+        far(9, twin_src, twin_dst, me_s, twin)
         ubar1 = net.pull_back(1, [rounded(gain * window[i]) for i in (0, 1)])
         for i in (0, 1):
             ubar_ref[i] = ubar1[i]
+
+    arrived(5, m_dst)
+    e_src[...] = jnp.stack(row.normal(slots_of(m_dst)), axis=1).astype(BF)
+    to_both_holders(7, e_src, e_dst)
+
+    @pl.when(active)
+    def _():
+        gain = win[2]
         arrived(4, d_dst)
         total = summed(d_dst)
         open_window(3, [total[0], total[1]], 1, edge2_src, edge2_dst)
@@ -438,30 +470,27 @@
         ubar0 = net.pull_back(0, mbar0)
         kept = w0 + (1.0 - w0)
         out = [
-            (w1 + kept * (1.0 - w1)) * window[i] + kept * ubar_ref[i] + ubar0[i]
-            for i in (0, 1)
+            (w1 + kept * (1.0 - w1)) * window[i] + kept * ubar_ref[i] + ubar0[i] for i in (0, 1)
         ]
         t_src[...] = jnp.stack([out[0][inner], out[1][inner]], axis=1).astype(BF)
         to_owners(6, t_src, t_dst)
 
-    arrived(5, m_dst)
-    e_src[...] = jnp.stack(row.normal(slots_of(m_dst)), axis=1).astype(BF)
-    to_holders(7, e_src, e_dst)
+    def image_block(base_ref):
+        total = summed(e_dst)
+        for i in (0, 1):
+            image_src[0, i] = (base_ref[i] - weight_ref[1] * total[i]).astype(BF)
+
+    arrived(7, e_dst)
+    pl.when(jnp.logical_not(active))(lambda: arrived(9, twin_dst))
+    whenever(active, lambda: image_block(twin_src), lambda: image_block(twin_dst))
+
+    @pl.loop(0, columns)
+    def _(x):
+        push(8, image_src.at[0], image_dst.at[me_x], me_s, me_hi * columns + x)
+
     arrived(6, t_dst)
     real, imag = row.expand(slots_of(t_dst))
     grad_ref[...] = packed([row.mask * real, row.mask * imag], half)
-
-    @pl.when(active)
-    def _():
-        arrived(7, e_dst)
-        total = summed(e_dst)
-        for i in (0, 1):
-            image_src[0, i] = (state_ref[i, inner] - weight_ref[1] * total[i]).astype(BF)
-
-        @pl.loop(0, coil_parts)
-        def _(q):
-            push(8, image_src.at[0], image_dst.at[me_x], me_s, q)
-
     arrived(8, image_dst)
     for x in range(columns):
         image_ref[x * block : x * block + block] = packed([image_dst[x, i].astype(F32) for i in (0, 1)], half)
@@ -472,12 +501,20 @@
         whenever(active, lambda: left(1, gain_ref.at[pl.ds(0, columns - 1)]), lambda: left(1, gain_ref))
     else:
         pl.when(jnp.logical_not(active))(lambda: left(1, gain_ref))
-    for index, src in ((3, y_src), (4, d_src), (7, e_src)):
+    for index, src in ((3, y_src), (4, d_src)):
         whenever(
             to_self,
             functools.partial(left, index, src.at[pl.ds(0, parts - 1)]),
             functools.partial(left, index, src),
         )
+
+    whenever(
+        me_x == my_block,
+        functools.partial(left, 7, e_dst.at[pl.ds(0, 2 * parts - 1)]),
+        functools.partial(left, 7, e_dst),
+    )
+    if columns > 1:
+        left(8, image_src)
 
     @pl.when(active)
     def _():
@@ -487,7 +524,7 @@
                 functools.partial(left, index, like.at[pl.ds(0, block * coil_parts - 1)]),
                 functools.partial(left, index, like),
             )
-        left(8, image_src)
+        left(9, twin_src)
         for which, src in ((0, edge_src), (1, edge2_src)):
             for side, there in ((0, me_x > 0), (1, me_x < columns - 1)):
                 def gone(which=which, side=side, src=src):
@@ -548,11 +585,12 @@
             pltpu.VMEM((2, 2, HALO, WIDE), BF), pltpu.VMEM((2, 2, HALO, WIDE), BF),
             pltpu.VMEM((5, high, WIDE), F32),
             owned, pair, owned, pair,
-            pltpu.VMEM((coil_parts - 1, 2, block, WIDE), BF),
+            pltpu.VMEM((max(columns - 1, 1), 2, block, WIDE), BF),
             pltpu.VMEM((columns, 2, block, WIDE), BF),
+            pltpu.VMEM((2, block, WIDE), F32), pltpu.VMEM((2, block, WIDE), F32),
             plane2, plane2,
             hidden, hidden, pltpu.VMEM((2, HID, high, WIDE), F32),
-            pltpu.SemaphoreType.DMA((9,)), pltpu.SemaphoreType.DMA((9,)),
+            pltpu.SemaphoreType.DMA((10,)), pltpu.SemaphoreType.DMA((10,)),
             pltpu.SemaphoreType.DMA((4,)), pltpu.SemaphoreType.DMA((4,)),
         ],
         compiler_params=pltpu.CompilerParams(collective_id=0, has_side_effects=True),

time: 95.3 us -> 86.9 us (0.912); the launches traced: 95 us -> 85.6 us
  Pallas kernels: 91.6 us -> 82.3 us
    pallas_call x1, Pallas kernels: 91.6 us -> 82.3 us  [body(): pl.pallas_call(functools.partial(cascade_kernel, parts, coil_parts), out_...]
where the time goes in v4:
time: 86.9 us; the launch traced here: 85.6 us
  Pallas kernels  82.3 us (95%)
  local copies, waits for them, and re-layouts  2.74 us (3%)
    pallas_call x1, Pallas kernels, body(): pl.pallas_call(functools.partial(cascade_kernel, parts, coil_parts), out_...  82.3 us
    unnamed x4, local copies, waits for them, and re-layouts  2.74 us

profile of v4, /device:TPU:1, one launch (start us, length us, event | category | flops | bytes accessed | tf_op | source)
XLA Modules:
  0.0 85.6 jit_solution(16870342491705542076)
XLA Ops:
  0.6 82.3 %cascade.1 = (f32[64,640]{1,0:T(8,128)}, f32[128,640]{1,0:T(8,128)}) custom-call(f32[2,9,2,18]{3,2,1,0:T(2,128)} %bitcast.13, f32[2,18]{1,0:T(2,128)} %bin_ref.1, f32[2,9,2,18]{3,2,1,0:T(2,128)} %kout_ref.1, f32[2,2]{1,0:T(2,128)} %bout_ref.1, f32[2]{0:T(128)} %weight_ref.1, bf16[2,64,640]{2,1,0:T(8,128)(2,1)} %bitcast.9, bf16[64,640]{1,0:T(8,128)(2,1)} %bitcast.12, ...), custom_call_target="tpu_custom_call" | custom-call | tf_op jit(solution)/shard_map/cascade/pallas_call | solution.py:565
  82.9 0.0 copy-start
  82.9 2.1 %copy.15 = f32[2,64,1,640]{3,2,1,0:T(1,128)} copy(f32[2,64,1,640]{3,1,0,2:T(8,128)} %bitcast.7) | data formatting | bytes 655360
  85.0 0.0 copy-done
  85.0 0.7 copy.17
Async XLA Ops:
  82.9 2.1 %copy-start = (f32[64,640]{1,0:T(8,128)S(1)}, f32[64,640]{1,0:T(8,128)}, u32[]{:S(2)}) copy-start(f32[64,640]{1,0:T(8,128)} %get-tuple-element.4) | copy-start | bytes 491524

commit v5 on v4

--- a/solution.py
+++ b/solution.py
@@ -214,7 +214,7 @@
     maps_in, cot_in, sampling_in, k_ref, c_ref, s_ref, zc_ref, zs_ref, load,
     maps_ref, cot_ref, gain_ref, cot_pad,
     maps_row, cot_row, gain_all,
-    y_src, y_dst, d_src, d_dst, e_src, e_dst,
+    y_src, y_dst, d_src, d_dst, e_src, share_dst, share_src, e_dst,
     edge_src, edge_dst, edge2_src, edge2_dst, win,
     m_src, m_dst, t_src, t_dst, image_src, image_dst, twin_src, twin_dst, state_ref, ubar_ref,
     taps_ref, hidden_ref, slope_ref,
@@ -343,16 +343,6 @@
             p = lax.rem(me_s + k, parts)
             far(index, src.at[p], dst.at[spot], p, holder(p, my_block))
 
-    def to_both_holders(index, src, dst):
-        for hi in (0, 1):
-            push(index, src.at[me_s], dst.at[spot], me_s, hi * columns + my_block)
-
-        @pl.loop(1, parts)
-        def _(k):
-            p = lax.rem(me_s + k, parts)
-            for hi in (0, 1):
-                far(index, src.at[p], dst.at[spot], p, hi * columns + my_block)
-
     def to_owners(index, src, dst):
         @pl.loop(0, block)
         def _(i):
@@ -385,13 +375,16 @@
         measured = row.mask * part
         start.append(measured - weighted * (measured - measured))
     images = row.inverse(*start)
+    to_section(2, cot_ref, cot_row)
     arrived(0, maps_row)
     row.take_maps(slots_of(maps_row))
     y_src[...] = jnp.stack(row.collect(*images), axis=1).astype(BF)
     to_holders(3, y_src, y_dst)
-    to_section(2, cot_ref, cot_row)
-
-    def exchange_edges(which, src, dst, count):
+    arrived(2, cot_row)
+    d_src[...] = jnp.stack(row.normal(slots_of(cot_row)), axis=1).astype(BF)
+    to_holders(4, d_src, d_dst)
+
+    def exchange_edges(which, src, dst):
         def link(side, coil):
             return pltpu.make_async_remote_copy(
                 src.at[side], dst.at[1 - side],
@@ -399,13 +392,8 @@
                 device_id={"section": me_s, "coil": coil}, device_id_type=pl.DeviceIdType.MESH,
             )
 
-        def coming(side):
-            pltpu.make_async_copy(dst.at[side], dst.at[side], edge_recv.at[which * 2 + side]).wait()
-
         pl.when(me_x > 0)(lambda: link(0, me_c - 1).start())
         pl.when(me_x < columns - 1)(lambda: link(1, me_c + 1).start())
-        pl.when(me_x > 0)(lambda: coming(0))
-        pl.when(me_x < columns - 1)(lambda: coming(1))
 
     def open_window(first, planes, which, src, dst):
         for i, plane in enumerate(planes):
@@ -413,8 +401,15 @@
             win[first + i, HALO : HALO + block] = plane
             src[0, i] = plane[:HALO].astype(BF)
             src[1, i] = plane[block - HALO :].astype(BF)
-        exchange_edges(which, src, dst, len(planes))
-        for i in range(len(planes)):
+        exchange_edges(which, src, dst)
+
+    def close_window(first, count, which, dst):
+        def coming(side):
+            pltpu.make_async_copy(dst.at[side], dst.at[side], edge_recv.at[which * 2 + side]).wait()
+
+        pl.when(me_x > 0)(lambda: coming(0))
+        pl.when(me_x < columns - 1)(lambda: coming(1))
+        for i in range(count):
             win[first + i, :HALO] = dst[0, i].astype(F32)
             win[first + i, HALO + block :] = dst[1, i].astype(F32)
 
@@ -429,39 +424,38 @@
         arrived(3, y_dst)
         total = summed(y_dst)
         open_window(0, [total[0], total[1], gains], 0, edge_src, edge_dst)
+        close_window(0, 3, 0, edge_dst)
         m0 = net.refine(0, [rounded(win[0]), rounded(win[1])])
         m_src[...] = jnp.stack([m0[0][inner], m0[1][inner]], axis=1).astype(BF)
         to_owners(5, m_src, m_dst)
         for i in (0, 1):
             state_ref[i] = win[i] + win[2] * m0[i]
-
-    arrived(2, cot_row)
-    d_src[...] = jnp.stack(row.normal(slots_of(cot_row)), axis=1).astype(BF)
-    to_holders(4, d_src, d_dst)
-
-    twin = (1 - me_hi) * columns + me_x
-
-    @pl.when(active)
-    def _():
         gain = win[2]
         m1 = net.refine(1, [rounded(state_ref[0]), rounded(state_ref[1])])
         for i in (0, 1):
             twin_src[i] = (state_ref[i] + gain * m1[i])[inner]
-        far(9, twin_src, twin_dst, me_s, twin)
+        far(9, twin_src, twin_dst, me_s, (1 - me_hi) * columns + me_x)
         ubar1 = net.pull_back(1, [rounded(gain * window[i]) for i in (0, 1)])
         for i in (0, 1):
             ubar_ref[i] = ubar1[i]
+        arrived(4, d_dst)
+        total = summed(d_dst)
+        open_window(3, [total[0], total[1]], 1, edge2_src, edge2_dst)
 
     arrived(5, m_dst)
     e_src[...] = jnp.stack(row.normal(slots_of(m_dst)), axis=1).astype(BF)
-    to_both_holders(7, e_src, e_dst)
+    share = parts // columns
+    near(7, e_src.at[pl.ds(me_x * share, share)], share_dst.at[me_x])
+
+    @pl.loop(1, columns)
+    def _(k):
+        x = lax.rem(me_x + k, columns)
+        far(7, e_src.at[pl.ds(x * share, share)], share_dst.at[me_x], me_s, me_hi * columns + x)
 
     @pl.when(active)
     def _():
         gain = win[2]
-        arrived(4, d_dst)
-        total = summed(d_dst)
-        open_window(3, [total[0], total[1]], 1, edge2_src, edge2_dst)
+        close_window(3, 2, 1, edge2_dst)
         w0 = weight_ref[0]
         w1 = weight_ref[1]
         mbar0 = [
@@ -473,14 +467,27 @@
             (w1 + kept * (1.0 - w1)) * window[i] + kept * ubar_ref[i] + ubar0[i] for i in (0, 1)
         ]
         t_src[...] = jnp.stack([out[0][inner], out[1][inner]], axis=1).astype(BF)
-        to_owners(6, t_src, t_dst)
+
+    arrived(7, share_dst)
+    share_src[...] = jnp.sum(share_dst[...].astype(F32), axis=0).astype(BF)
+    spot2 = me_hi * block + lax.rem(me_s, block)
+
+    @pl.loop(0, share)
+    def _(k):
+        j = lax.rem(me_s + k, share)
+        p = me_x * share + j
+        for hi in (0, 1):
+            push(10, share_src.at[j], e_dst.at[spot2], p, hi * columns + my_block)
+
+    pl.when(active)(lambda: to_owners(6, t_src, t_dst))
 
     def image_block(base_ref):
-        total = summed(e_dst)
+        halves = e_dst[...].astype(F32)
+        total = jnp.swapaxes(halves[:block] + halves[block:], 0, 1)
         for i in (0, 1):
             image_src[0, i] = (base_ref[i] - weight_ref[1] * total[i]).astype(BF)
 
-    arrived(7, e_dst)
+    arrived(10, e_dst)
     pl.when(jnp.logical_not(active))(lambda: arrived(9, twin_dst))
     whenever(active, lambda: image_block(twin_src), lambda: image_block(twin_dst))
 
@@ -490,7 +497,7 @@
 
     arrived(6, t_dst)
     real, imag = row.expand(slots_of(t_dst))
-    grad_ref[...] = packed([row.mask * real, row.mask * imag], half)
+    grad_ref[:, 0, :] = packed([row.mask * real, row.mask * imag], half)
     arrived(8, image_dst)
     for x in range(columns):
         image_ref[x * block : x * block + block] = packed([image_dst[x, i].astype(F32) for i in (0, 1)], half)
@@ -508,17 +515,19 @@
             functools.partial(left, index, src),
         )
 
+    if columns > 1:
+        left(7, share_dst.at[pl.ds(0, columns - 1)])
     whenever(
-        me_x == my_block,
-        functools.partial(left, 7, e_dst.at[pl.ds(0, 2 * parts - 1)]),
-        functools.partial(left, 7, e_dst),
+        jnp.logical_and(me_x == my_block, me_x == lax.div(me_s, share)),
+        functools.partial(left, 10, e_dst.at[pl.ds(0, 2 * share - 1)]),
+        functools.partial(left, 10, e_dst),
     )
     if columns > 1:
         left(8, image_src)
 
     @pl.when(active)
     def _():
-        for index, like in ((5, e_dst), (6, e_dst)):
+        for index, like in ((5, y_dst), (6, y_dst)):
             whenever(
                 to_self,
                 functools.partial(left, index, like.at[pl.ds(0, block * coil_parts - 1)]),
@@ -566,7 +575,7 @@
         functools.partial(cascade_kernel, parts, coil_parts),
         out_shape=(
             jax.ShapeDtypeStruct((rows, width_two), F32),
-            jax.ShapeDtypeStruct((coils * slots, width_two), F32),
+            jax.ShapeDtypeStruct((coils * slots, 1, width_two), F32),
         ),
         in_specs=[SMEM] * 5 + [pl.BlockSpec(memory_space=pl.ANY)] * 8,
         out_specs=(VMEM, VMEM),
@@ -580,7 +589,10 @@
             pltpu.VMEM((slots, coils, width_two), BF),
             pair,
             pltpu.VMEM((coil_parts, block, WIDE), BF),
-            pair, gathered, pair, gathered, pair, gathered,
+            pair, gathered, pair, gathered, pair,
+            pltpu.VMEM((columns, parts // columns, 2, WIDE), BF),
+            pltpu.VMEM((parts // columns, 2, WIDE), BF),
+            pltpu.VMEM((2 * block, 2, WIDE), BF),
             pltpu.VMEM((2, 3, HALO, WIDE), BF), pltpu.VMEM((2, 3, HALO, WIDE), BF),
             pltpu.VMEM((2, 2, HALO, WIDE), BF), pltpu.VMEM((2, 2, HALO, WIDE), BF),
             pltpu.VMEM((5, high, WIDE), F32),
@@ -590,7 +602,7 @@
             pltpu.VMEM((2, block, WIDE), F32), pltpu.VMEM((2, block, WIDE), F32),
             plane2, plane2,
             hidden, hidden, pltpu.VMEM((2, HID, high, WIDE), F32),
-            pltpu.SemaphoreType.DMA((10,)), pltpu.SemaphoreType.DMA((10,)),
+            pltpu.SemaphoreType.DMA((11,)), pltpu.SemaphoreType.DMA((11,)),
             pltpu.SemaphoreType.DMA((4,)), pltpu.SemaphoreType.DMA((4,)),
         ],
         compiler_params=pltpu.CompilerParams(collective_id=0, has_side_effects=True),

time: 86.9 us -> 87.7 us (level); the launches traced: 85.6 us -> 87.5 us
  Pallas kernels: 82.3 us -> 84.4 us
    pallas_call x1, Pallas kernels: 82.3 us -> 84.4 us  [body(): pl.pallas_call(functools.partial(cascade_kernel, parts, coil_parts), out_...]
where the time goes in v5:
time: 87.7 us; the launch traced here: 87.5 us
  Pallas kernels  84.4 us (96%)
  local copies, waits for them, and re-layouts  2.37 us (3%)
    pallas_call x1, Pallas kernels, body(): pl.pallas_call(functools.partial(cascade_kernel, parts, coil_parts), out_...  84.4 us
    unnamed x4, local copies, waits for them, and re-layouts  2.37 us

profile of v5, /device:TPU:1, one launch (start us, length us, event | category | flops | bytes accessed | tf_op | source)
XLA Modules:
  0.0 87.5 jit_solution(13271100147673229936)
XLA Ops:
  0.6 84.4 %cascade.1 = (f32[64,640]{1,0:T(8,128)}, f32[128,1,640]{2,1,0:T(1,128)}) custom-call(f32[2,9,2,18]{3,2,1,0:T(2,128)} %bitcast.13, f32[2,18]{1,0:T(2,128)} %bin_ref.1, f32[2,9,2,18]{3,2,1,0:T(2,128)} %kout_ref.1, f32[2,2]{1,0:T(2,128)} %bout_ref.1, f32[2]{0:T(128)} %weight_ref.1, bf16[2,64,640]{2,1,0:T(8,128)(2,1)} %bitcast.9, bf16[64,640]{1,0:T(8,128)(2,1)} %bitcast.12, ...), custom_call_target="tpu_custom_call" | custom-call | tf_op jit(solution)/shard_map/cascade/pallas_call | solution.py:574
  85.1 0.0 copy-start
  85.1 1.6 %copy.17 = f32[1,64,640]{2,1,0:T(8,128)} copy(f32[1,64,640]{2,1,0:T(8,128)} %bitcast.8) | data formatting | bytes 327680
  86.7 0.0 copy-done
  86.7 0.7 copy.18
Async XLA Ops:
  85.1 1.7 %copy-start = (f32[128,1,640]{2,1,0:T(1,128)S(1)}, f32[128,1,640]{2,1,0:T(1,128)}, u32[]{:S(2)}) copy-start(f32[128,1,640]{2,1,0:T(1,128)} %get-tuple-element.5) | copy-start | bytes 983044

commit v6 on v5

--- a/solution.py
+++ b/solution.py
@@ -199,6 +199,16 @@
             self.taps[k] = self.mix(self.hidden, lambda o: self.kin[t, tap, channel, o], None)
 
         return [rounded(x) for x in self.gather_taps(-1)]
+
+
+def in_groups(first, last, act):
+    count = last - first
+    group = next(n for n in (9, 8, 7, 5, 3, 1) if count % n == 0)
+
+    @pl.loop(0, count // group)
+    def _(g):
+        for k in range(group):
+            act(first + g * group + k)
 
 
 def clear(first_ref, second_ref, side):
@@ -270,13 +280,8 @@
             barrier, 1, device_id={"section": section, "coil": coil}, device_id_type=pl.DeviceIdType.MESH
         )
 
-    @pl.loop(1, parts)
-    def _(k):
-        greet(lax.rem(me_s + k, parts), me_c)
-
-    @pl.loop(1, coil_parts)
-    def _(k):
-        greet(me_s, lax.rem(me_c + k, coil_parts))
+    in_groups(1, parts, lambda k: greet(lax.rem(me_s + k, parts), me_c))
+    in_groups(1, coil_parts, lambda k: greet(me_s, lax.rem(me_c + k, coil_parts)))
 
     loads = [
         pltpu.make_async_copy(src, dst, load.at[i])
@@ -319,10 +324,11 @@
     def to_section(index, src, dst):
         near(index, src.at[me_s], dst.at[me_s])
 
-        @pl.loop(1, parts)
-        def _(k):
+        def send_to(k):
             p = lax.rem(me_s + k, parts)
             far(index, src.at[p], dst.at[me_s], p, me_c)
+
+        in_groups(1, parts, send_to)
 
     to_section(0, maps_ref, maps_row)
 
@@ -330,6 +336,11 @@
     def _(x):
         push(1, gain_ref.at[x], gain_all.at[me_c], me_s, holder(me_s, x))
 
+    @pl.loop(0, block)
+    def _(k):
+        r = me_x * block + lax.rem(me_s + k, block)
+        push(2, cot_ref.at[r], cot_row.at[me_s], r, me_c)
+
     pl.when(me_x == 0)(lambda: clear(edge_dst, edge2_dst, 0))
     pl.when(me_x == columns - 1)(lambda: clear(edge_dst, edge2_dst, 1))
 
@@ -338,18 +349,18 @@
     def to_holders(index, src, dst):
         push(index, src.at[me_s], dst.at[spot], me_s, holder(me_s, my_block))
 
-        @pl.loop(1, parts)
-        def _(k):
+        def send_to(k):
             p = lax.rem(me_s + k, parts)
             far(index, src.at[p], dst.at[spot], p, holder(p, my_block))
+
+        in_groups(1, parts, send_to)
 
     def to_owners(index, src, dst):
         @pl.loop(0, block)
         def _(i):
             push(index, src.at[i], dst.at[me_s], me_x * block + i, me_c)
 
-            @pl.loop(1, coil_parts)
-            def _(k):
+            for k in range(1, coil_parts):
                 far(index, src.at[i], dst.at[me_s], me_x * block + i, lax.rem(me_c + k, coil_parts))
 
     def slots_of(ref):
@@ -375,12 +386,23 @@
         measured = row.mask * part
         start.append(measured - weighted * (measured - measured))
     images = row.inverse(*start)
-    to_section(2, cot_ref, cot_row)
     arrived(0, maps_row)
     row.take_maps(slots_of(maps_row))
     y_src[...] = jnp.stack(row.collect(*images), axis=1).astype(BF)
     to_holders(3, y_src, y_dst)
     arrived(2, cot_row)
+
+    def relays():
+        return [
+            pltpu.make_async_remote_copy(
+                cot_row, cot_row, send.at[10 + k], recv.at[2],
+                device_id={"section": me_s, "coil": me_hi * columns + lax.rem(me_x + k, columns)},
+                device_id_type=pl.DeviceIdType.MESH,
+            )
+            for k in range(1, columns)
+        ]
+
+    pl.when(me_x == my_block)(lambda: [copy.start() for copy in relays()] and None)
     d_src[...] = jnp.stack(row.normal(slots_of(cot_row)), axis=1).astype(BF)
     to_holders(4, d_src, d_dst)
 
@@ -503,7 +525,13 @@
         image_ref[x * block : x * block + block] = packed([image_dst[x, i].astype(F32) for i in (0, 1)], half)
 
     left(0, maps_ref.at[pl.ds(0, parts - 1)])
-    left(2, cot_ref.at[pl.ds(0, parts - 1)])
+    whenever(
+        me_x == my_block,
+        functools.partial(left, 2, cot_ref.at[pl.ds(0, block - 1)]),
+        functools.partial(left, 2, cot_ref.at[pl.ds(0, block)]),
+    )
+    for k in range(1, columns):
+        pl.when(me_x == my_block)(functools.partial(left, 10 + k, cot_row))
     if columns > 1:
         whenever(active, lambda: left(1, gain_ref.at[pl.ds(0, columns - 1)]), lambda: left(1, gain_ref))
     else:
@@ -602,7 +630,7 @@
             pltpu.VMEM((2, block, WIDE), F32), pltpu.VMEM((2, block, WIDE), F32),
             plane2, plane2,
             hidden, hidden, pltpu.VMEM((2, HID, high, WIDE), F32),
-            pltpu.SemaphoreType.DMA((11,)), pltpu.SemaphoreType.DMA((11,)),
+            pltpu.SemaphoreType.DMA((10 + columns,)), pltpu.SemaphoreType.DMA((11,)),
             pltpu.SemaphoreType.DMA((4,)), pltpu.SemaphoreType.DMA((4,)),
         ],
         compiler_params=pltpu.CompilerParams(collective_id=0, has_side_effects=True),

time: 87.7 us -> 84.6 us (0.965)
  Pallas kernels: 84.4 us -> 81.4 us
    pallas_call x1, Pallas kernels: 84.4 us -> 81.4 us  [body(): pl.pallas_call(functools.partial(cascade_kernel, parts, coil_parts), out_...]
where the time goes in v6:
time: 84.6 us; the launch traced here: 84.4 us
  Pallas kernels  81.4 us (96%)
  local copies, waits for them, and re-layouts  2.37 us (3%)
    pallas_call x1, Pallas kernels, body(): pl.pallas_call(functools.partial(cascade_kernel, parts, coil_parts), out_...  81.4 us
    unnamed x4, local copies, waits for them, and re-layouts  2.37 us

profile of v6, /device:TPU:1, one launch (start us, length us, event | category | flops | bytes accessed | tf_op | source)
XLA Modules:
  0.0 84.4 jit_solution(15326235423166458507)
XLA Ops:
  0.6 81.4 %cascade.1 = (f32[64,640]{1,0:T(8,128)}, f32[128,1,640]{2,1,0:T(1,128)}) custom-call(f32[2,9,2,18]{3,2,1,0:T(2,128)} %bitcast.13, f32[2,18]{1,0:T(2,128)} %bin_ref.1, f32[2,9,2,18]{3,2,1,0:T(2,128)} %kout_ref.1, f32[2,2]{1,0:T(2,128)} %bout_ref.1, f32[2]{0:T(128)} %weight_ref.1, bf16[2,64,640]{2,1,0:T(8,128)(2,1)} %bitcast.9, bf16[64,640]{1,0:T(8,128)(2,1)} %bitcast.12, ...), custom_call_target="tpu_custom_call" | custom-call | tf_op jit(solution)/shard_map/cascade/pallas_call | solution.py:602
  82.0 0.0 copy-start
  82.0 1.6 %copy.17 = f32[1,64,640]{2,1,0:T(8,128)} copy(f32[1,64,640]{2,1,0:T(8,128)} %bitcast.8) | data formatting | bytes 327680
  83.7 0.0 copy-done
  83.7 0.7 copy.18
Async XLA Ops:
  82.0 1.7 %copy-start = (f32[128,1,640]{2,1,0:T(1,128)S(1)}, f32[128,1,640]{2,1,0:T(1,128)}, u32[]{:S(2)}) copy-start(f32[128,1,640]{2,1,0:T(1,128)} %get-tuple-element.5) | copy-start | bytes 983044
